TPU v7x, 256 devices: a whole 4x4x8 slice. The times are simulated.
256 devices in a mesh: gx: 16 (over y, x), gy: 16 (over z, core).
Axes of the slice: x: 4, y: 4, z: 8, core: 2. Of those that a mesh axis runs over, the one named last changes fastest.
Arguments:
- velocity: float32 [3, 2, 2048, 2048], P(None, None, 'gx', 'gy'), may hold values from -8 to 8
- diffusion: float32 [2, 2048, 2048], P(None, 'gx', 'gy'), may hold values from 16384 to 262144
Outputs:
- new_velocity: float32 [3, 2, 2048, 2048], P(None, None, 'gx', 'gy')
All inputs are finite; a program needn't handle non-finite values.
Results may differ from a plain program's by a relative error of at most 0.000024.
Values sent between devices are 32-bit elements; how exact they have to be, the bound alone decides.
No kernel may reach another device: no remote copies, remote signals or barrier semaphores. Data moves between devices by JAX's collectives and lax.ppermute only.
A program may use at most 64 MiB of HBM per device.

v0:
```python
import jax
import jax.numpy as jnp
from jax import lax
from jax.sharding import PartitionSpec as P

courant = 0.25


def prefix_2(part, axis, combine, identity, reverse):
    count = lax.axis_size(axis)
    place = lax.axis_index(axis)
    ahead = count - 1 - place if reverse else place
    gathered = jax.tree.map(lambda a: lax.all_gather(a, axis), part)
    state = jax.tree.map(lambda a, e: jnp.zeros_like(a) + jnp.asarray(e, a.dtype), part, identity)

    def one(hop, state):
        source = count - 1 - hop if reverse else hop
        return combine(
            state, jax.tree.map(lambda a: lax.dynamic_index_in_dim(a, source, 0, False), gathered)
        )

    return lax.fori_loop(0, ahead, one, state)


def padded_2(block, sides, width):
    for axis, dim in sides:
        count = lax.axis_size(axis)
        forward = [(i, i + 1) for i in range(count - 1)]
        backward = [(target, source) for source, target in forward]
        low = lax.ppermute(
            lax.slice_in_dim(block, block.shape[dim] - width, None, axis=dim), axis, forward
        )
        high = lax.ppermute(lax.slice_in_dim(block, 0, width, axis=dim), axis, backward)
        block = jnp.concatenate([low, block, high], axis=dim)
    return block


def compose(former, latter):
    top_left = latter[0] * former[0] + latter[1] * former[2]
    top_right = latter[0] * former[1] + latter[1] * former[3]
    low_left = latter[2] * former[0] + latter[3] * former[2]
    low_right = latter[2] * former[1] + latter[3] * former[3]
    carried = latter[4] * former[4]
    row_first = latter[5] * former[0] + latter[6] * former[2] + latter[4] * former[5]
    row_second = latter[5] * former[1] + latter[6] * former[3] + latter[4] * former[6]
    factor = 1.0 / (jnp.abs(top_left) + jnp.abs(top_right) + jnp.abs(low_left) + jnp.abs(low_right))
    return (
        top_left * factor,
        top_right * factor,
        low_left * factor,
        low_right * factor,
        carried * factor,
        row_first * factor,
        row_second * factor,
    )


def combine_affine(former, latter):
    return (latter[0] * former[0], latter[0] * former[1] + latter[1])


def neutral_of(shape):
    ones = jnp.ones(shape, jnp.float32)
    zeros = jnp.zeros(shape, jnp.float32)
    return (ones, zeros, zeros, ones, ones, zeros, zeros)


def forward(source, lower_face, upper_face):

    def advance(carry, entries):
        low_now, high_now, src_now = entries
        below = jnp.broadcast_to(low_now[None], src_now.shape)
        above = jnp.broadcast_to(high_now[None], src_now.shape)
        element = (
            below,
            jnp.ones_like(src_now),
            below,
            1.0 + above,
            below,
            jnp.zeros_like(src_now),
            src_now,
        )
        joined = compose(carry, element)
        return (joined, joined)

    unused, prefix = lax.scan(
        advance, neutral_of(source.shape[1:]), (lower_face, upper_face, source), unroll=8
    )
    return prefix


def eliminate(prefix, share_in, value_in):
    numer = prefix[0] * share_in + prefix[1]
    denom = prefix[2] * share_in + prefix[3]
    upper_q = prefix[5] * share_in + prefix[6] + prefix[4] * value_in
    return (numer / denom, upper_q / denom)


def backward(keep_part, value_part):

    def retreat(carry, entries):
        keep_now, value_now = entries
        slope = keep_now * carry[0]
        offset = value_now + keep_now * carry[1]
        return ((slope, offset), (slope, offset))

    start = (
        jnp.ones(keep_part.shape[1:], jnp.float32),
        jnp.zeros(keep_part.shape[1:], jnp.float32),
    )
    unused, suffix = lax.scan(retreat, start, (keep_part, value_part), reverse=True, unroll=8)
    return suffix


def entering(before):
    scale_in = before[2] + before[3]
    return ((before[0] + before[1]) / scale_in, (before[5] + before[6]) / scale_in)


def chain_x(source, lower_face, upper_face):
    prefix = forward(source, lower_face, upper_face)
    ends = tuple((leaf[-1] for leaf in prefix))
    before = prefix_2(
        (ends[0], ends[1], ends[2], ends[3], ends[4], ends[5], ends[6]),
        "gx",
        compose,
        neutral_of(ends[0].shape),
        False,
    )
    share_in, value_in = entering(before)
    share, value = eliminate(prefix, share_in, value_in)
    suffix = backward(1.0 - share, value)
    starts = (suffix[0][0], suffix[1][0])
    behind = prefix_2(
        (starts[0], starts[1]),
        "gx",
        combine_affine,
        (jnp.ones_like(starts[0]), jnp.zeros_like(starts[1])),
        True,
    )
    return suffix[0] * behind[1][None] + suffix[1]


def chain_y(source, lower_face, upper_face):
    prefix = forward(source, lower_face, upper_face)
    ends = tuple((leaf[-1] for leaf in prefix))
    before = prefix_2(
        (ends[0], ends[1], ends[2], ends[3], ends[4], ends[5], ends[6]),
        "gy",
        compose,
        neutral_of(ends[0].shape),
        False,
    )
    share_in, value_in = entering(before)
    share, value = eliminate(prefix, share_in, value_in)
    suffix = backward(1.0 - share, value)
    starts = (suffix[0][0], suffix[1][0])
    behind = prefix_2(
        (starts[0], starts[1]),
        "gy",
        combine_affine,
        (jnp.ones_like(starts[0]), jnp.zeros_like(starts[1])),
        True,
    )
    return suffix[0] * behind[1][None] + suffix[1]


def local(velocity, diffusion):
    stacked = jnp.concatenate([velocity, diffusion[None]], 0)
    padded = padded_2(stacked, (("gx", 2), ("gy", 3)), 1)
    grad_x = padded[:3, :, 2:, 1:-1] - padded[:3, :, :-2, 1:-1]
    grad_y = padded[:3, :, 1:-1, 2:] - padded[:3, :, 1:-1, :-2]
    source = velocity - 0.5 * courant * (velocity[0] * grad_x + velocity[1] * grad_y)
    viscous = padded[3]
    lower_x = 0.5 * (viscous[:, :-2, 1:-1] + diffusion)
    upper_x = 0.5 * (viscous[:, 2:, 1:-1] + diffusion)
    lower_y = 0.5 * (viscous[:, 1:-1, :-2] + diffusion)
    upper_y = 0.5 * (viscous[:, 1:-1, 2:] + diffusion)
    source_lead = jnp.transpose(source, (2, 0, 1, 3))
    lower_xl = jnp.transpose(lower_x, (1, 0, 2))
    upper_xl = jnp.transpose(upper_x, (1, 0, 2))
    lower_yl = jnp.transpose(lower_y, (2, 0, 1))
    upper_yl = jnp.transpose(upper_y, (2, 0, 1))
    middle = chain_x(source_lead, lower_xl, upper_xl)
    middle_lead = jnp.transpose(middle, (3, 1, 2, 0))
    result = chain_y(middle_lead, lower_yl, upper_yl)
    return jnp.transpose(result, (1, 2, 3, 0))


def solution(mesh):
    in_specs = (P(None, None, "gx", "gy"), P(None, "gx", "gy"))
    out_specs = P(None, None, "gx", "gy")
    return jax.shard_map(local, mesh=mesh, in_specs=in_specs, out_specs=out_specs, check_vma=False)
```

profile of v0, /device:TPU:1, one launch (start us, length us, event | category | flops | bytes accessed | tf_op | source)
XLA Modules:
  0.0 507.6 jit_solution(17637147052700925927)
XLA Ops:
  0.9 3.9 collective-permute-start
  4.8 1.3 collective-permute-start.1
  6.1 3.0 collective-permute-done.1
  9.7 5.5 %collective-permute-start.2 = (f32[4,2,130,1]{2,0,3,1:T(4,128)S(1)}, f32[4,2,130,1]{2,0,3,1:T(4,128)S(1)}, u32[]{:S(2)}, u32[]{:S(2)}) collective-permute-start(f32[4,2,130,1]{2,0,3,1:T(4,128)S(1)} %copy.65), channel_id=1, source_target_pairs={{0,1},{1,2},{2,3},{3,4},{4,5},{5,6},{6,7},{7,8},{8,9},{9,10},{10,1... | collective-permute-start | bytes 12488 | tf_op jit(solution)/shard_map/ppermute | solution.py:30
  15.6 1.9 collective-permute-start.3
  18.0 2.6 collective-permute-done.3
  21.0 0.9 fusion.176
  23.1 89.3 %while.192 = (s32[]{:T(128)}, f32[3,2,128]{2,1,0:T(2,128)S(1)}, f32[3,2,128]{2,1,0:T(2,128)S(1)}, f32[3,2,128]{2,1,0:T(2,128)S(1)}, f32[3,2,128]{2,1,0:T(2,128)S...) while((s32[]{:T(128)}, f32[3,2,128]{2,1,0:T(2,128)S(1)}, ...), condition=%wide.region_1.2_spmd.clone, body=%wide.region_0.1_spmd.clone.sunk | while | flops 273155 | bytes 1203728 | solution.py:86
  23.1 1.0 constant_dynamic-slice_fusion.88
  24.2 1.0 constant_dynamic-slice_fusion.86
  28.6 1.2 constant_dynamic-slice_fusion.88
  29.9 1.0 constant_dynamic-slice_fusion.86
  34.4 1.2 constant_dynamic-slice_fusion.88
  35.6 1.0 constant_dynamic-slice_fusion.86
  40.1 1.3 constant_dynamic-slice_fusion.88
  41.4 1.0 constant_dynamic-slice_fusion.86
  45.8 1.0 constant_dynamic-slice_fusion.88
  46.8 1.0 constant_dynamic-slice_fusion.86
  51.3 1.2 constant_dynamic-slice_fusion.88
  52.6 1.0 constant_dynamic-slice_fusion.86
  57.0 1.2 constant_dynamic-slice_fusion.88
  58.3 1.0 constant_dynamic-slice_fusion.86
  62.8 1.2 constant_dynamic-slice_fusion.88
  64.0 1.0 constant_dynamic-slice_fusion.86
  68.5 1.0 constant_dynamic-slice_fusion.88
  69.5 1.0 constant_dynamic-slice_fusion.86
  74.0 1.0 constant_dynamic-slice_fusion.88
  75.0 1.0 constant_dynamic-slice_fusion.86
  79.5 1.0 constant_dynamic-slice_fusion.88
  80.5 1.0 constant_dynamic-slice_fusion.86
  85.0 1.0 constant_dynamic-slice_fusion.88
  86.0 1.0 constant_dynamic-slice_fusion.86
  90.5 1.0 constant_dynamic-slice_fusion.88
  91.5 1.0 constant_dynamic-slice_fusion.86
  96.0 1.0 constant_dynamic-slice_fusion.88
  97.0 1.0 constant_dynamic-slice_fusion.86
  101.5 1.0 constant_dynamic-slice_fusion.88
  102.5 1.0 constant_dynamic-slice_fusion.86
  107.0 1.0 constant_dynamic-slice_fusion.88
  108.0 1.0 constant_dynamic-slice_fusion.86
  113.8 20.2 %all_gather.54 = f32[16,3,2,128]{3,2,1,0:T(2,128)S(1)} all-gather(f32[1,3,2,128]{3,2,1,0:T(2,128)S(1)} %slice.734), channel_id=1, replica_groups=mesh['gx'=16,'gy'=16] {'gx'}, dimensions={0}, use_global_device_ids=true | all-gather | bytes 52224 | tf_op jit(solution)/shard_map/all_gather | solution.py:13
  134.7 16.9 %all_gather.55 = f32[16,3,2,128]{3,2,1,0:T(2,128)S(1)} all-gather(f32[1,3,2,128]{3,2,1,0:T(2,128)S(1)} %slice.735), channel_id=1, replica_groups=mesh['gx'=16,'gy'=16] {'gx'}, dimensions={0}, use_global_device_ids=true | all-gather | bytes 52224 | tf_op jit(solution)/shard_map/all_gather | solution.py:13
  152.3 16.4 %all_gather.56 = f32[16,3,2,128]{3,2,1,0:T(2,128)S(1)} all-gather(f32[1,3,2,128]{3,2,1,0:T(2,128)S(1)} %slice.736), channel_id=1, replica_groups=mesh['gx'=16,'gy'=16] {'gx'}, dimensions={0}, use_global_device_ids=true | all-gather | bytes 52224 | tf_op jit(solution)/shard_map/all_gather | solution.py:13
  169.3 16.9 %all_gather.57 = f32[16,3,2,128]{3,2,1,0:T(2,128)S(1)} all-gather(f32[1,3,2,128]{3,2,1,0:T(2,128)S(1)} %slice.737), channel_id=1, replica_groups=mesh['gx'=16,'gy'=16] {'gx'}, dimensions={0}, use_global_device_ids=true | all-gather | bytes 52224 | tf_op jit(solution)/shard_map/all_gather | solution.py:13
  187.0 16.8 %all_gather.58 = f32[16,3,2,128]{3,2,1,0:T(2,128)S(1)} all-gather(f32[1,3,2,128]{3,2,1,0:T(2,128)S(1)} %slice.738), channel_id=1, replica_groups=mesh['gx'=16,'gy'=16] {'gx'}, dimensions={0}, use_global_device_ids=true | all-gather | bytes 52224 | tf_op jit(solution)/shard_map/all_gather | solution.py:13
  204.5 17.0 %all_gather.59 = f32[16,3,2,128]{3,2,1,0:T(2,128)S(1)} all-gather(f32[1,3,2,128]{3,2,1,0:T(2,128)S(1)} %slice.739), channel_id=1, replica_groups=mesh['gx'=16,'gy'=16] {'gx'}, dimensions={0}, use_global_device_ids=true | all-gather | bytes 52224 | tf_op jit(solution)/shard_map/all_gather | solution.py:13
  222.1 16.4 %all_gather.60 = f32[16,3,2,128]{3,2,1,0:T(2,128)S(1)} all-gather(f32[1,3,2,128]{3,2,1,0:T(2,128)S(1)} %slice.740), channel_id=1, replica_groups=mesh['gx'=16,'gy'=16] {'gx'}, dimensions={0}, use_global_device_ids=true | all-gather | bytes 52224 | tf_op jit(solution)/shard_map/all_gather | solution.py:13
  238.6 2.3 add_divide_fusion.20
  241.6 5.5 %while.193 = (s32[]{:T(128)}, f32[3,2,128]{2,1,0:T(2,128)S(1)}, f32[3,2,128]{2,1,0:T(2,128)S(1)}, f32[16,8,3,2,128]{4,1,0,3,2:T(8,128)S(1)}, f32[16,8,3,2,128]{4...) while((s32[]{:T(128)}, f32[3,2,128]{2,1,0:T(2,128)S(1)}, ...), condition=%wide.region_5.6_spmd.clone, body=%wide.region_4.5_spmd.clone.sunk | while | flops 23817 | bytes 322916 | solution.py:111
  247.0 18.1 %all_gather.61 = f32[16,3,2,128]{3,2,1,0:T(2,128)S(1)} all-gather(f32[1,3,2,128]{3,2,1,0:T(2,128)S(1)} %bitcast.1389), channel_id=1, replica_groups=mesh['gx'=16,'gy'=16] {'gx'}, dimensions={0}, use_global_device_ids=true | all-gather | bytes 52224 | tf_op jit(solution)/shard_map/all_gather | solution.py:13
  265.1 16.6 %all_gather.62 = f32[16,3,2,128]{3,2,1,0:T(2,128)S(1)} all-gather(f32[1,3,2,128]{3,2,1,0:T(2,128)S(1)} %bitcast.1390), channel_id=1, replica_groups=mesh['gx'=16,'gy'=16] {'gx'}, dimensions={0}, use_global_device_ids=true | all-gather | bytes 52224 | tf_op jit(solution)/shard_map/all_gather | solution.py:13
  284.2 17.9 %while.194 = (s32[]{:T(128)}, f32[3,2,128]{2,1,0:T(2,128)S(1)}, f32[3,2,128]{2,1,0:T(2,128)S(1)}, f32[3,2,128]{2,1,0:T(2,128)S(1)}, f32[3,2,128]{2,1,0:T(2,128)S...) while((s32[]{:T(128)}, f32[3,2,128]{2,1,0:T(2,128)S(1)}, ...), condition=%wide.region_9.10_spmd.clone, body=%wide.region_8.9_spmd.clone.sunk | while | flops 273155 | bytes 1166780 | solution.py:86
  303.6 67.6 %all_gather.63 = f32[16,3,2,128]{3,2,1,0:T(2,128)S(1)} all-gather(f32[1,3,2,128]{3,2,1,0:T(2,128)S(1)} %slice.743), channel_id=1, replica_groups=mesh['gx'=16,'gy'=16] {'gy'}, dimensions={0}, use_global_device_ids=true | all-gather | bytes 52224 | tf_op jit(solution)/shard_map/all_gather | solution.py:13
  371.8 15.2 %all_gather.64 = f32[16,3,2,128]{3,2,1,0:T(2,128)S(1)} all-gather(f32[1,3,2,128]{3,2,1,0:T(2,128)S(1)} %slice.744), channel_id=1, replica_groups=mesh['gx'=16,'gy'=16] {'gy'}, dimensions={0}, use_global_device_ids=true | all-gather | bytes 52224 | tf_op jit(solution)/shard_map/all_gather | solution.py:13
  387.7 15.3 %all_gather.65 = f32[16,3,2,128]{3,2,1,0:T(2,128)S(1)} all-gather(f32[1,3,2,128]{3,2,1,0:T(2,128)S(1)} %slice.745), channel_id=1, replica_groups=mesh['gx'=16,'gy'=16] {'gy'}, dimensions={0}, use_global_device_ids=true | all-gather | bytes 52224 | tf_op jit(solution)/shard_map/all_gather | solution.py:13
  403.6 15.2 %all_gather.66 = f32[16,3,2,128]{3,2,1,0:T(2,128)S(1)} all-gather(f32[1,3,2,128]{3,2,1,0:T(2,128)S(1)} %slice.746), channel_id=1, replica_groups=mesh['gx'=16,'gy'=16] {'gy'}, dimensions={0}, use_global_device_ids=true | all-gather | bytes 52224 | tf_op jit(solution)/shard_map/all_gather | solution.py:13
  419.5 15.4 %all_gather.67 = f32[16,3,2,128]{3,2,1,0:T(2,128)S(1)} all-gather(f32[1,3,2,128]{3,2,1,0:T(2,128)S(1)} %slice.747), channel_id=1, replica_groups=mesh['gx'=16,'gy'=16] {'gy'}, dimensions={0}, use_global_device_ids=true | all-gather | bytes 52224 | tf_op jit(solution)/shard_map/all_gather | solution.py:13
  435.6 15.2 %all_gather.68 = f32[16,3,2,128]{3,2,1,0:T(2,128)S(1)} all-gather(f32[1,3,2,128]{3,2,1,0:T(2,128)S(1)} %slice.748), channel_id=1, replica_groups=mesh['gx'=16,'gy'=16] {'gy'}, dimensions={0}, use_global_device_ids=true | all-gather | bytes 52224 | tf_op jit(solution)/shard_map/all_gather | solution.py:13
  451.5 15.3 %all_gather.69 = f32[16,3,2,128]{3,2,1,0:T(2,128)S(1)} all-gather(f32[1,3,2,128]{3,2,1,0:T(2,128)S(1)} %slice.749), channel_id=1, replica_groups=mesh['gx'=16,'gy'=16] {'gy'}, dimensions={0}, use_global_device_ids=true | all-gather | bytes 52224 | tf_op jit(solution)/shard_map/all_gather | solution.py:13
  467.0 2.4 add_divide_fusion.18
  469.5 5.5 %while.195 = (s32[]{:T(128)}, f32[3,2,128]{2,1,0:T(2,128)S(1)}, f32[3,2,128]{2,1,0:T(2,128)S(1)}, f32[16,8,3,2,128]{4,1,0,3,2:T(8,128)S(1)}, f32[16,8,3,2,128]{4...) while((s32[]{:T(128)}, f32[3,2,128]{2,1,0:T(2,128)S(1)}, ...), condition=%wide.region_13.14_spmd.clone, body=%wide.region_12.13_spmd.clone.sunk | while | flops 23817 | bytes 322916 | solution.py:111
  475.0 16.5 %all_gather.70 = f32[16,3,2,128]{3,2,1,0:T(2,128)S(1)} all-gather(f32[1,3,2,128]{3,2,1,0:T(2,128)S(1)} %bitcast.1391), channel_id=1, replica_groups=mesh['gx'=16,'gy'=16] {'gy'}, dimensions={0}, use_global_device_ids=true | all-gather | bytes 52224 | tf_op jit(solution)/shard_map/all_gather | solution.py:13
  491.4 14.6 %all_gather.71 = f32[16,3,2,128]{3,2,1,0:T(2,128)S(1)} all-gather(f32[1,3,2,128]{3,2,1,0:T(2,128)S(1)} %bitcast.1392), channel_id=1, replica_groups=mesh['gx'=16,'gy'=16] {'gy'}, dimensions={0}, use_global_device_ids=true | all-gather | bytes 52224 | tf_op jit(solution)/shard_map/all_gather | solution.py:13
  506.6 0.9 copy.88
  (2180 shorter events, 95.5 us)
Async XLA Ops:
  0.0 9.1 %copy-start = (f32[3,2,128,128]{3,2,1,0:T(8,128)S(1)}, f32[3,2,128,128]{3,2,1,0:T(8,128)}, u32[]{:S(2)}) copy-start(f32[3,2,128,128]{3,2,1,0:T(8,128)} %param.18) | copy-start | bytes 1179652
  0.0 9.1 %copy-start.1 = (f32[2,128,128]{2,1,0:T(8,128)S(1)}, f32[2,128,128]{2,1,0:T(8,128)}, u32[]{:S(2)}) copy-start(f32[2,128,128]{2,1,0:T(8,128)} %param.19) | copy-start | bytes 393220
  0.9 5.2 %collective-permute-start = (f32[4,2,1,128]{3,2,1,0:T(1,128)S(1)}, f32[4,2,1,128]{3,2,1,0:T(1,128)S(1)}, u32[]{:S(2)}, u32[]{:S(2)}) collective-permute-start(f32[4,2,1,128]{3,2,1,0:T(1,128)S(1)} %get-tuple-element.1857), channel_id=1, source_target_pairs={{0,16},{16,32},{32,48},{48,64},{64,80},{80,96},{96,112},{112,128},... | collective-permute-start | bytes 12296 | tf_op jit(solution)/shard_map/ppermute | solution.py:30
  4.8 4.4 collective-permute-start.1
  9.7 8.0 %collective-permute-start.2 = (f32[4,2,130,1]{2,0,3,1:T(4,128)S(1)}, f32[4,2,130,1]{2,0,3,1:T(4,128)S(1)}, u32[]{:S(2)}, u32[]{:S(2)}) collective-permute-start(f32[4,2,130,1]{2,0,3,1:T(4,128)S(1)} %copy.65), channel_id=1, source_target_pairs={{0,1},{1,2},{2,3},{3,4},{4,5},{5,6},{6,7},{7,8},{8,9},{9,10},{10,1... | collective-permute-start | bytes 12488 | tf_op jit(solution)/shard_map/ppermute | solution.py:30
  15.6 5.0 collective-permute-start.3
  25.2 0.7 copy-start.23
  25.9 0.7 copy-start.21
  25.9 0.7 copy-start.20
  30.9 0.7 copy-start.23
  31.6 0.7 copy-start.21
  31.6 0.7 copy-start.20
  36.6 0.7 copy-start.23
  37.3 0.7 copy-start.21
  37.3 0.7 copy-start.20
  42.4 0.7 copy-start.23
  43.1 0.7 copy-start.21
  43.1 0.7 copy-start.20
  47.9 0.7 copy-start.23
  48.6 0.7 copy-start.21
  48.6 0.7 copy-start.20
  53.6 0.7 copy-start.23
  54.3 0.7 copy-start.21
  54.3 0.7 copy-start.20
  59.3 0.7 copy-start.23
  60.0 0.7 copy-start.20
  65.0 0.7 copy-start.23
  65.7 0.7 copy-start.21
  65.7 0.7 copy-start.20
  70.5 0.7 copy-start.23
  71.2 0.7 copy-start.20
  76.0 0.7 copy-start.23
  76.7 0.7 copy-start.20
  81.5 0.7 copy-start.23
  82.2 0.7 copy-start.20
  87.0 0.7 copy-start.23
  87.7 0.7 copy-start.20
  92.5 0.7 copy-start.23
  93.2 0.7 copy-start.20
  98.0 0.7 copy-start.23
  98.7 0.7 copy-start.20
  103.5 0.7 copy-start.23
  104.2 0.7 copy-start.20
  109.0 0.7 copy-start.23
  109.7 0.7 copy-start.20
  112.4 0.7 copy-start.2
  112.4 21.6 %copy-start.4 = (f32[16,8,3,2,128]{4,3,2,1,0:T(2,128)}, f32[16,8,3,2,128]{4,3,2,1,0:T(2,128)S(1)}, u32[]{:S(2)}) copy-start(f32[16,8,3,2,128]{4,3,2,1,0:T(2,128)S(1)} %get-tuple-element.892) | copy-start | bytes 1179652
  112.4 39.2 %copy-start.5 = (f32[16,8,3,2,128]{4,3,2,1,0:T(2,128)}, f32[16,8,3,2,128]{4,3,2,1,0:T(2,128)S(1)}, u32[]{:S(2)}) copy-start(f32[16,8,3,2,128]{4,3,2,1,0:T(2,128)S(1)} %get-tuple-element.893) | copy-start | bytes 1179652
  112.4 56.2 %copy-start.6 = (f32[16,8,3,2,128]{4,3,2,1,0:T(2,128)}, f32[16,8,3,2,128]{4,3,2,1,0:T(2,128)S(1)}, u32[]{:S(2)}) copy-start(f32[16,8,3,2,128]{4,3,2,1,0:T(2,128)S(1)} %get-tuple-element.894) | copy-start | bytes 1179652
  112.4 73.9 %copy-start.8 = (f32[16,8,3,2,128]{4,3,2,1,0:T(2,128)}, f32[16,8,3,2,128]{4,3,2,1,0:T(2,128)S(1)}, u32[]{:S(2)}) copy-start(f32[16,8,3,2,128]{4,3,2,1,0:T(2,128)S(1)} %get-tuple-element.895) | copy-start | bytes 1179652
  112.4 91.3 %copy-start.9 = (f32[16,8,3,2,128]{4,3,2,1,0:T(2,128)}, f32[16,8,3,2,128]{4,3,2,1,0:T(2,128)S(1)}, u32[]{:S(2)}) copy-start(f32[16,8,3,2,128]{4,3,2,1,0:T(2,128)S(1)} %get-tuple-element.896) | copy-start | bytes 1179652
  112.4 109.0 %copy-start.7 = (f32[16,8,3,2,128]{4,3,2,1,0:T(2,128)}, f32[16,8,3,2,128]{4,3,2,1,0:T(2,128)S(1)}, u32[]{:S(2)}) copy-start(f32[16,8,3,2,128]{4,3,2,1,0:T(2,128)S(1)} %get-tuple-element.897) | copy-start | bytes 1179652
  187.0 51.6 %copy-start.3 = (f32[16,8,3,2,128]{4,3,2,1,0:T(2,128)S(1)}, f32[16,8,3,2,128]{4,3,2,1,0:T(2,128)}, u32[]{:S(2)}) copy-start(f32[16,8,3,2,128]{4,3,2,1,0:T(2,128)} %copy-done.2) | copy-start | bytes 1179652
  240.9 0.7 copy-start.19
  283.5 0.7 copy-start.18
  283.5 0.7 copy-start.22
  302.1 0.7 copy-start.10
  302.1 69.0 %copy-start.12 = (f32[16,8,3,2,128]{4,3,2,1,0:T(2,128)}, f32[16,8,3,2,128]{4,3,2,1,0:T(2,128)S(1)}, u32[]{:S(2)}) copy-start(f32[16,8,3,2,128]{4,3,2,1,0:T(2,128)S(1)} %get-tuple-element.908) | copy-start | bytes 1179652
  302.2 84.9 %copy-start.13 = (f32[16,8,3,2,128]{4,3,2,1,0:T(2,128)}, f32[16,8,3,2,128]{4,3,2,1,0:T(2,128)S(1)}, u32[]{:S(2)}) copy-start(f32[16,8,3,2,128]{4,3,2,1,0:T(2,128)S(1)} %get-tuple-element.909) | copy-start | bytes 1179652
  302.2 100.8 %copy-start.14 = (f32[16,8,3,2,128]{4,3,2,1,0:T(2,128)}, f32[16,8,3,2,128]{4,3,2,1,0:T(2,128)S(1)}, u32[]{:S(2)}) copy-start(f32[16,8,3,2,128]{4,3,2,1,0:T(2,128)S(1)} %get-tuple-element.910) | copy-start | bytes 1179652
  302.2 116.7 %copy-start.16 = (f32[16,8,3,2,128]{4,3,2,1,0:T(2,128)}, f32[16,8,3,2,128]{4,3,2,1,0:T(2,128)S(1)}, u32[]{:S(2)}) copy-start(f32[16,8,3,2,128]{4,3,2,1,0:T(2,128)S(1)} %get-tuple-element.911) | copy-start | bytes 1179652
  302.2 132.8 %copy-start.17 = (f32[16,8,3,2,128]{4,3,2,1,0:T(2,128)}, f32[16,8,3,2,128]{4,3,2,1,0:T(2,128)S(1)}, u32[]{:S(2)}) copy-start(f32[16,8,3,2,128]{4,3,2,1,0:T(2,128)S(1)} %get-tuple-element.912) | copy-start | bytes 1179652
  302.2 148.6 %copy-start.15 = (f32[16,8,3,2,128]{4,3,2,1,0:T(2,128)}, f32[16,8,3,2,128]{4,3,2,1,0:T(2,128)S(1)}, u32[]{:S(2)}) copy-start(f32[16,8,3,2,128]{4,3,2,1,0:T(2,128)S(1)} %get-tuple-element.913) | copy-start | bytes 1179652
  419.5 47.4 %copy-start.11 = (f32[16,8,3,2,128]{4,3,2,1,0:T(2,128)S(1)}, f32[16,8,3,2,128]{4,3,2,1,0:T(2,128)}, u32[]{:S(2)}) copy-start(f32[16,8,3,2,128]{4,3,2,1,0:T(2,128)} %copy-done.10) | copy-start | bytes 1179652
  (9 other events, 6.0 us)
where the time goes:
time: 511 us; the launch traced here: 508 us
  blocking collectives  345 us (68%)
  local copies, waits for them, and re-layouts  85.1 us (17%)
  other arithmetic  49.5 us (10%)
  starting transfers between devices  12.7 us (2%)
  loops' own time  8.55 us (2%)
  waiting for transfers between devices  5.62 us (1%)
    all_gather x18, blocking collectives, prefix_2(): gathered = jax.tree.map(lambda a: lax.all_gather(a, axis), part)  345 us
    slice x96, local copies, waits for them, and re-layouts, forward(): lax.scan(advance, neutral_of(source.shape[1:]), (lower_face, upper_face,...  36.4 us
    while x416, other arithmetic  30.8 us
    while x1056, local copies, waits for them, and re-layouts  28.8 us
  transfers between devices with their start and end apart: 4, of which 2 were waited for; matrix products, arithmetic and copies ran while one was open for 0% of the time, Pallas kernels for 0%

commit v1 on v0

v1 whole, which is shorter than its diff:
```python
import jax
import jax.numpy as jnp
from jax import lax
from jax.experimental import pallas as pl
from jax.experimental.pallas import tpu as pltpu
from jax.sharding import PartitionSpec as P


COURANT = 0.25
HALF = 0.5 * COURANT
SEG = 16
PLANES = 2
COMPS = 3
LANES = 128
ROWS_X = 40
ROWS_Y = 24
ROW_G, ROW_EL, ROW_ER, ROW_DHI, ROW_DLO = 0, 2, 4, 6, 8
ROW_JL, ROW_JR, ROW_VLO, ROW_VHI = 10, 16, 22, 28

f32 = jnp.float32
VMEM = pltpu.VMEM


def sub_iota():
    return lax.broadcasted_iota(jnp.int32, (8, LANES), 0)


def lane_iota():
    return lax.broadcasted_iota(jnp.int32, (8, LANES), 1)


def ahead(x, count):
    return pltpu.roll(x, 8 - count, 0)


def after(x, count):
    return pltpu.roll(x, count, 0)


def strided(ref, lead, t):
    return ref[lead, pl.ds(t, 8, stride=SEG), :]


def factor(cells, first, coef_ref, tree_ref, head_ref, plane):
    row = sub_iota()
    last = row == 7
    faces = [0.5 * (cells[t] + cells[t + 1]) for t in range(SEG - 1)]
    faces.append(0.5 * (cells[SEG - 1] + ahead(cells[0], 1)))
    leak_l = 1.0 + jnp.where(jnp.logical_and(row == 0, first), 0.5 * cells[0], 0.0)
    g = faces[0]
    leak_r = jnp.ones_like(g)
    for t in range(1, SEG):
        f = faces[t]
        inv = 1.0 / (g + f + leak_r)
        a = g * inv
        b = f * inv
        if t == SEG - 1:
            inv = jnp.where(last, 0.0, inv)
            g = jnp.where(last, g, a * f)
            a = jnp.where(last, 0.0, a)
            b = jnp.where(last, 1.0, b)
            leak_l = leak_l + a * leak_r
            leak_r = b * leak_r
        else:
            g = a * f
            leak_l = leak_l + a * leak_r
            leak_r = 1.0 + b * leak_r
        coef_ref[plane, 0, t] = a
        coef_ref[plane, 1, t] = b
        coef_ref[plane, 2, t] = inv
    for level in range(3):
        count = 1 << level
        g_next = ahead(g, count)
        leak = leak_r + ahead(leak_l, count)
        inv = 1.0 / (g + g_next + leak)
        a = g * inv
        b = g_next * inv
        g = a * g_next
        leak_l = leak_l + a * leak
        leak_r = ahead(leak_r, count) + b * leak
        tree_ref[plane, level, 0] = a
        tree_ref[plane, level, 1] = b
        tree_ref[plane, level, 2] = inv
    for base, value in ((ROW_G, g), (ROW_EL, leak_l), (ROW_ER, leak_r)):
        head_ref[base + plane : base + plane + 1, :] = value[0:1]
    head_ref[ROW_DHI + plane : ROW_DHI + plane + 1, :] = cells[SEG - 1][7:8]
    head_ref[ROW_DLO + plane : ROW_DLO + plane + 1, :] = cells[0][0:1]


def condense(sources, coef_ref, tree_ref, q_ref, qtree_ref, plane, comp):
    k = comp * PLANES + plane
    left = sources[0]
    right = sources[1]
    for t in range(1, SEG):
        q_ref[k, t] = coef_ref[plane, 2, t] * right
        left = left + coef_ref[plane, 0, t] * right
        right = coef_ref[plane, 1, t] * right
        if t < SEG - 1:
            right = right + sources[t + 1]
    for level in range(3):
        count = 1 << level
        j = right + ahead(left, count)
        left = left + tree_ref[plane, level, 0] * j
        right = ahead(right, count) + tree_ref[plane, level, 1] * j
        qtree_ref[k, level] = tree_ref[plane, level, 2] * j
    return left, right


def unfold(low, high, coef_ref, tree_ref, q_ref, qtree_ref, plane, comp, store):
    k = comp * PLANES + plane
    row = sub_iota()

    def mid(level, lo, hi):
        return (
            tree_ref[plane, level, 0] * lo
            + tree_ref[plane, level, 1] * hi
            + qtree_ref[k, level]
        )

    for level in (2, 1, 0):
        count = 1 << level
        between = mid(level, low, high)
        late = (row & count) != 0
        low = jnp.where(late, after(between, count), low)
        high = jnp.where(late, after(high, count), between)
    store(0, low)
    cell = high
    for t in range(SEG - 1, 0, -1):
        cell = (
            coef_ref[plane, 0, t] * low
            + q_ref[k, t]
            + coef_ref[plane, 1, t] * cell
        )
        store(t, cell)


def solve_ends(ring_ref, rows, me, count, plane, advect):
    row = sub_iota()

    def take(which, half, shift=0):
        slot = me + 8 * half + shift
        return ring_ref[pl.ds(slot * rows + which + plane, 8, stride=rows), :]

    halves = []
    for half in (0, 1):
        place = (me + 8 * half + row) & (count - 1)
        wall = place == count - 1
        g = take(ROW_G, half)
        leak_l = take(ROW_EL, half)
        leak_r = take(ROW_ER, half)
        f = 0.5 * (take(ROW_DHI, half) + jnp.where(wall, 0.0, take(ROW_DLO, half, 1)))
        inv = 1.0 / (g + f + leak_r)
        a = g * inv
        b = f * inv
        through = a * f
        leak_l = leak_l + a * leak_r
        leak_l = jnp.where(wall, leak_l + through, leak_l)
        own = (a, b, inv)
        g = jnp.where(wall, 0.0, through)
        leak_r = jnp.where(wall, 0.0, b * leak_r)
        b_cut = jnp.where(wall, 0.0, b)
        currents = []
        if advect:
            up_lo = jnp.where(place == 0, 0.0, HALF * take(ROW_VLO, half))
            up_hi = jnp.where(wall, 0.0, HALF * take(ROW_VHI, half))
        for comp in range(COMPS):
            left = take(ROW_JL + comp * PLANES, half)
            right = take(ROW_JR + comp * PLANES, half)
            if advect:
                same = after(take(ROW_VHI + comp * PLANES, half), 1)
                other = after(take(ROW_VHI + comp * PLANES, 1 - half), 1)
                left = left + up_lo * jnp.where(row == 0, other, same)
                right = right - up_hi * take(ROW_VLO + comp * PLANES, half, 1)
            q = inv * right
            left = left + a * right
            currents.append((left, b_cut * right, q))
        levels = []
        for level in range(3):
            step = 1 << level
            g_next = ahead(g, step)
            leak = leak_r + ahead(leak_l, step)
            inv_n = 1.0 / (g + g_next + leak)
            a_n = g * inv_n
            b_n = g_next * inv_n
            g = a_n * g_next
            leak_l = leak_l + a_n * leak
            leak_r = ahead(leak_r, step) + b_n * leak
            levels.append((a_n, b_n, inv_n))
        merged = []
        for left, right, q in currents:
            terms = []
            for level in range(3):
                step = 1 << level
                a_n, b_n, inv_n = levels[level]
                j = right + ahead(left, step)
                left = left + a_n * j
                right = ahead(right, step) + b_n * j
                terms.append(inv_n * j)
            merged.append((left, right, q, terms))
        halves.append((own, g, leak_l, leak_r, levels, merged))
    own, g, leak_l, leak_r, levels, merged = halves[0]
    _, g_next, leak_l_next, leak_r_next, _, merged_next = halves[1]
    leak = leak_r + leak_l_next
    inv = 1.0 / (g + g_next + leak)
    a = g * inv
    b = g_next * inv
    total = 1.0 / (leak_l + a * leak + leak_r_next + b * leak)
    at_wall = me == count - 1
    ends = []
    for comp in range(COMPS):
        left, right, q, terms = merged[comp]
        left_next, right_next, _, _ = merged_next[comp]
        j = right + left_next
        first = (left + a * j + right_next + b * j) * total
        high = (a + b) * first + inv * j
        for level in (2, 1, 0):
            a_n, b_n, _ = levels[level]
            high = a_n * first + b_n * high + terms[level]
        high = jnp.where(at_wall, 0.0, high)
        ends.append((first, own[0] * first + own[1] * high + q))
    return ends


def fill_ring(got_ref, ring_ref, rows, count):
    size = rows * count
    block = got_ref[...]
    ring_ref[0:size, :] = block
    ring_ref[size : 2 * size, :] = block


def send_all(page_ref, out_ref, rows, count):
    page = page_ref[...]
    for i in range(count):
        out_ref[i * rows : (i + 1) * rows, :] = page


def edges_kernel(velocity_ref, low_ref, high_ref):
    for k in range(COMPS * PLANES):
        comp, plane = divmod(k, PLANES)
        turned = jnp.transpose(velocity_ref[comp, plane])
        low_ref[k : k + 1, :] = turned[0:1]
        high_ref[k : k + 1, :] = turned[LANES - 1 : LANES]
    low_ref[6:8, :] = jnp.zeros((2, LANES), f32)
    high_ref[6:8, :] = jnp.zeros((2, LANES), f32)


def matrix_kernel(diffusion_ref, cx_ref, tx_ref, hx_ref, cy_ref, ty_ref, hy_ref, turn_ref):
    first_x = lax.axis_index("gx") == 0
    first_y = lax.axis_index("gy") == 0
    for plane in range(PLANES):
        turn_ref[plane] = jnp.transpose(diffusion_ref[plane])
        cells = [strided(diffusion_ref, plane, t) for t in range(SEG)]
        factor(cells, first_x, cx_ref, tx_ref, hx_ref, plane)
        cells = [strided(turn_ref, plane, t) for t in range(SEG)]
        factor(cells, first_y, cy_ref, ty_ref, hy_ref, plane)
    for ref in (hx_ref, hy_ref):
        ref[10:16, :] = jnp.zeros((6, LANES), f32)


def source_kernel(count, velocity_ref, from_low_ref, from_high_ref, coef_ref, tree_ref, head_ref,
                  out_ref, q_ref, qtree_ref, edge_ref, halo_ref, page_ref):
    me_y = lax.axis_index("gy")
    count_y = lax.axis_size("gy")
    row = sub_iota()
    lane = lane_iota()
    low = jnp.where(me_y == 0, 0.0, from_low_ref[...])
    high = jnp.where(me_y == count_y - 1, 0.0, from_high_ref[...])
    edge_ref[0:8, :] = low
    edge_ref[8:16, :] = high
    edge_ref[16:, :] = jnp.zeros((LANES - 16, LANES), f32)
    halo_ref[...] = jnp.transpose(edge_ref[...])
    page_ref[0:16, :] = head_ref[...]
    page_ref[32:, :] = jnp.zeros((ROWS_X - 32, LANES), f32)
    for plane in range(PLANES):
        cells = [
            [velocity_ref[comp, plane, pl.ds(t, 8, stride=SEG), :] for t in range(SEG)]
            for comp in range(COMPS)
        ]
        halos = [halo_ref[pl.ds(t, 8, stride=SEG), :] for t in range(SEG)]
        for comp in range(COMPS):
            k = comp * PLANES + plane
            own = cells[comp]
            sources = []
            for t in range(SEG):
                if t < SEG - 1:
                    fore = own[t + 1]
                else:
                    fore = jnp.where(row == 7, 0.0, ahead(own[0], 1))
                if t > 0:
                    back = own[t - 1]
                else:
                    back = jnp.where(row == 0, 0.0, after(own[SEG - 1], 1))
                lo = jnp.broadcast_to(halos[t][:, k : k + 1], (8, LANES))
                hi = jnp.broadcast_to(halos[t][:, 8 + k : 9 + k], (8, LANES))
                right = jnp.where(lane == LANES - 1, hi, pltpu.roll(own[t], LANES - 1, 1))
                left = jnp.where(lane == 0, lo, pltpu.roll(own[t], 1, 1))
                sources.append(
                    own[t]
                    - HALF * (cells[0][t] * (fore - back) + cells[1][t] * (right - left))
                )
            left, right = condense(sources, coef_ref, tree_ref, q_ref, qtree_ref, plane, comp)
            page_ref[ROW_JL + k : ROW_JL + k + 1, :] = left[0:1]
            page_ref[ROW_JR + k : ROW_JR + k + 1, :] = right[0:1]
            page_ref[ROW_VLO + k : ROW_VLO + k + 1, :] = own[0][0:1]
            page_ref[ROW_VHI + k : ROW_VHI + k + 1, :] = own[SEG - 1][7:8]
    send_all(page_ref, out_ref, ROWS_X, count)


def middle_kernel(count_x, count_y, got_ref, cx_ref, tx_ref, qx_ref, qtx_ref, cy_ref, ty_ref, hy_ref,
                  out_ref, q_ref, qtree_ref, ring_ref, plane_ref, turn_ref, page_ref):
    me = lax.axis_index("gx")
    fill_ring(got_ref, ring_ref, ROWS_X, count_x)
    page_ref[0:16, :] = hy_ref[...]
    page_ref[16:, :] = jnp.zeros((ROWS_Y - 16, LANES), f32)
    for plane in range(PLANES):
        ends = solve_ends(ring_ref, ROWS_X, me, count_x, plane, True)
        for comp in range(COMPS):
            k = comp * PLANES + plane
            low, high = ends[comp]

            def store(t, value):
                plane_ref[k, pl.ds(t, 8, stride=SEG), :] = value

            unfold(low, high, cx_ref, tx_ref, qx_ref, qtx_ref, plane, comp, store)
            turn_ref[k] = jnp.transpose(plane_ref[k])
            sources = [strided(turn_ref, k, t) for t in range(SEG)]
            left, right = condense(sources, cy_ref, ty_ref, q_ref, qtree_ref, plane, comp)
            page_ref[ROW_JL + k : ROW_JL + k + 1, :] = left[0:1]
            page_ref[ROW_JR + k : ROW_JR + k + 1, :] = right[0:1]
    send_all(page_ref, out_ref, ROWS_Y, count_y)


def final_kernel(count, got_ref, coef_ref, tree_ref, q_ref, qtree_ref, out_ref, ring_ref, plane_ref):
    me = lax.axis_index("gy")
    fill_ring(got_ref, ring_ref, ROWS_Y, count)
    for plane in range(PLANES):
        ends = solve_ends(ring_ref, ROWS_Y, me, count, plane, False)
        for comp in range(COMPS):
            k = comp * PLANES + plane
            low, high = ends[comp]

            def store(t, value):
                plane_ref[k, pl.ds(t, 8, stride=SEG), :] = value

            unfold(low, high, coef_ref, tree_ref, q_ref, qtree_ref, plane, comp, store)
            out_ref[comp, plane] = jnp.transpose(plane_ref[k])


def shape(*dims):
    return jax.ShapeDtypeStruct(dims, f32)


def call(kernel, outs, scratch, cost, *args):
    spec = pl.BlockSpec(memory_space=VMEM)
    return pl.pallas_call(
        kernel,
        out_shape=outs,
        in_specs=[spec] * len(args),
        out_specs=jax.tree.map(lambda _: spec, outs),
        scratch_shapes=scratch,
        cost_estimate=pl.CostEstimate(flops=cost, bytes_accessed=1 << 19, transcendentals=0),
        compiler_params=pltpu.CompilerParams(vmem_limit_bytes=8 << 20),
    )(*args)


def local(velocity, diffusion):
    from functools import partial

    count_x = lax.axis_size("gx")
    count_y = lax.axis_size("gy")
    tile = (8, LANES)
    n = COMPS * PLANES
    low, high = call(edges_kernel, (shape(*tile), shape(*tile)), [], 1 << 17, velocity)
    from_low = lax.ppermute(high, "gy", [(i, (i + 1) % count_y) for i in range(count_y)])
    from_high = lax.ppermute(low, "gy", [((i + 1) % count_y, i) for i in range(count_y)])
    coef = shape(PLANES, 3, SEG, *tile)
    tree = shape(PLANES, 3, 3, *tile)
    head = shape(16, LANES)
    q_all = shape(n, SEG, *tile)
    q_tree = shape(n, 3, *tile)
    block = VMEM((n, LANES, LANES), f32)
    cx, tx, hx, cy, ty, hy = call(
        matrix_kernel,
        (coef, tree, head, coef, tree, head),
        [VMEM((PLANES, LANES, LANES), f32)],
        1 << 21,
        diffusion,
    )
    sent, qx, qtx = call(
        partial(source_kernel, count_x),
        (shape(count_x * ROWS_X, LANES), q_all, q_tree),
        [VMEM((LANES, LANES), f32), VMEM((LANES, LANES), f32), VMEM((ROWS_X, LANES), f32)],
        1 << 22,
        velocity, from_low, from_high, cx, tx, hx,
    )
    got = lax.all_to_all(sent.reshape(count_x, ROWS_X, LANES), "gx", 0, 0)
    sent, qy, qty = call(
        partial(middle_kernel, count_x, count_y),
        (shape(count_y * ROWS_Y, LANES), q_all, q_tree),
        [VMEM((2 * count_x * ROWS_X, LANES), f32), block, block, VMEM((ROWS_Y, LANES), f32)],
        1 << 22,
        got.reshape(-1, LANES), cx, tx, qx, qtx, cy, ty, hy,
    )
    got = lax.all_to_all(sent.reshape(count_y, ROWS_Y, LANES), "gy", 0, 0)
    return call(
        partial(final_kernel, count_y),
        shape(COMPS, PLANES, LANES, LANES),
        [VMEM((2 * count_y * ROWS_Y, LANES), f32), block],
        1 << 22,
        got.reshape(-1, LANES), cy, ty, qy, qty,
    )


def solution(mesh):
    in_specs = (P(None, None, "gx", "gy"), P(None, "gx", "gy"))
    out_specs = P(None, None, "gx", "gy")
    return jax.shard_map(local, mesh=mesh, in_specs=in_specs, out_specs=out_specs, check_vma=False)
```

time: 511 us -> 44.7 us (0.09)
  blocking collectives: 345 us -> 34.7 us
  local copies, waits for them, and re-layouts: 85.1 us -> 1.9 us
  other arithmetic: 49.5 us -> 0 us
  starting transfers between devices: 12.7 us -> 3.24 us
  loops' own time: 8.55 us -> 0 us
    all_gather x18 -> x0, blocking collectives: 345 us -> none  [prefix_2(): gathered = jax.tree.map(lambda a: lax.all_gather(a, axis), part)]
    slice x117 -> x0, local copies, waits for them, and re-layouts: 46.8 us -> none  [the longest x96 36.4 us: forward(): lax.scan(advance, neutral_of(source.shape[1:]), (lower_face, upper_face,...]
    all_to_all x0 -> x2, blocking collectives: none -> 34.7 us  [the longest x1 20.2 us: local(): got = lax.all_to_all(sent.reshape(count_y, ROWS_Y, LANES), 'gy', 0, 0)]
    while x416 -> x0, other arithmetic: 30.8 us -> none
    while x1056 -> x0, local copies, waits for them, and re-layouts: 28.8 us -> none
    concatenate x33 -> x0, other arithmetic: 10.2 us -> none  [the longest x32 10.1 us: forward(): lax.scan(advance, neutral_of(source.shape[1:]), (lower_face, upper_face,...]
    ppermute x4 -> x2, starting transfers between devices: 12.7 us -> 3.24 us  [the longest x1 3.03 us: local(): lax.ppermute(high, 'gy', [(i, (i + 1) % count_y) for i in range(count_y)])]
    another operation x8 -> x0, loops' own time: 8.55 us -> none  [the longest x2 5.12 us: forward(): lax.scan(advance, neutral_of(source.shape[1:]), (lower_face, upper_face,...]
  transfers between devices with their start and end apart: 4 -> 2, of which waited for: 2 -> 1; matrix products, arithmetic and copies ran while one was open for 0% -> 0% of each run, Pallas kernels for 0% -> 1%
where the time goes in v1:
time: 44.7 us; the launch traced here: 44.5 us
  blocking collectives  34.7 us (78%)
  starting transfers between devices  3.24 us (7%)
  Pallas kernels  3.04 us (7%)
  local copies, waits for them, and re-layouts  1.9 us (4%)
  waiting for transfers between devices  1.6 us (4%)
    all_to_all x1, blocking collectives, local(): got = lax.all_to_all(sent.reshape(count_y, ROWS_Y, LANES), 'gy', 0, 0)  20.2 us
    all_to_all x1, blocking collectives, local(): got = lax.all_to_all(sent.reshape(count_x, ROWS_X, LANES), 'gx', 0, 0)  14.4 us
    pallas_call x5, Pallas kernels, call(): pl.pallas_call(kernel, out_shape=outs, in_specs=[spec] * len(args), out_s...  3.04 us
    ppermute x1, starting transfers between devices, local(): lax.ppermute(high, 'gy', [(i, (i + 1) % count_y) for i in range(count_y)])  3.03 us
    unnamed x6, local copies, waits for them, and re-layouts  1.9 us
    ppermute x1, waiting for transfers between devices, local(): lax.ppermute(low, 'gy', [((i + 1) % count_y, i) for i in range(count_y)])  1.6 us
  transfers between devices with their start and end apart: 2, of which 1 were waited for; matrix products, arithmetic and copies ran while one was open for 0% of the time, Pallas kernels for 1%

profile of v1, /device:TPU:1, one launch (start us, length us, event | category | flops | bytes accessed | tf_op | source)
XLA Modules:
  0.0 44.5 jit_solution(7987508542831116897)
XLA Ops:
  0.0 0.0 copy-start
  0.0 1.0 %copy-done = f32[3,2,128,128]{3,2,1,0:T(8,128)S(1)} copy-done((f32[3,2,128,128]{3,2,1,0:T(8,128)S(1)}, f32[3,2,128,128]{3,2,1,0:T(8,128)}, u32[]{:S(2)}) %copy-start) | copy-done | bytes 393240
  1.0 0.0 copy-start.1
  1.0 0.2 shard_map.28
  1.2 3.0 %collective-permute-start = (f32[8,128]{1,0:T(8,128)S(1)}, f32[8,128]{1,0:T(8,128)S(1)}, u32[]{:S(2)}, u32[]{:S(2)}) collective-permute-start(f32[8,128]{1,0:T(8,128)S(1)} %get-tuple-element.19), channel_id=1, source_target_pairs={{0,1},{1,2},{2,3},{3,4},{4,5},{5,6},{6,7},{7,8},{8,9},{9,10},{10,1... | collective-permute-start | bytes 12296 | tf_op jit(solution)/shard_map/ppermute | solution.py:374
  4.2 0.2 collective-permute-start.1
  4.4 0.0 copy-start.2
  4.4 0.9 %copy-done.2 = f32[2,128,128]{2,1,0:T(8,128)S(1)} copy-done((f32[2,128,128]{2,1,0:T(8,128)S(1)}, f32[2,128,128]{2,1,0:T(8,128)}, u32[]{:S(2)}) %copy-start.2) | copy-done | bytes 131096
  5.3 0.3 shard_map.29
  5.6 0.0 collective-permute-done.from_low_ref
  5.6 1.6 %collective-permute-done.1.from_high_ref = f32[8,128]{1,0:T(8,128)S(1)} collective-permute-done((f32[8,128]{1,0:T(8,128)S(1)}, f32[8,128]{1,0:T(8,128)S(1)}, u32[]{:S(2)}, u32[]{:S(2)}) %collective-permute-start.1) | collective-permute-done | bytes 4128 | tf_op jit(solution)/shard_map/ppermute | solution.py:375
  7.2 0.0 copy-done.1
  7.2 0.9 %shard_map.30 = (f32[640,128]{1,0:T(8,128)S(1)}, f32[6,16,8,128]{3,2,1,0:T(8,128)S(1)}, f32[6,3,8,128]{3,2,1,0:T(8,128)S(1)}) custom-call(f32[3,2,128,128]{3,2,1,0:T(8,128)S(1)} %copy-done.1, f32[8,128]{1,0:T(8,128)S(1)} %collective-permute-done.from_low_ref, f32[8,128]{1,0:T(8,128)S(1)} %collective-permute-done.1.from_high_ref, ...), custom_call_target="tpu_custom_call" | custom-call | flops 4194304 | bytes 524288 | tf_op jit(solution)/shard_map/pallas_call | solution.py:355
  8.1 14.4 %all_to_all.10 = f32[16,40,128]{2,1,0:T(8,128)S(1)} all-to-all(f32[16,40,128]{2,1,0:T(8,128)S(1)} %bitcast.6), channel_id=1, replica_groups=mesh['gx'=16,'gy'=16] {'gx'}, dimensions={0} | all-to-all | bytes 655360 | tf_op jit(solution)/shard_map/all_to_all | solution.py:396
  22.5 0.6 %shard_map.31 = (f32[384,128]{1,0:T(8,128)S(1)}, f32[6,16,8,128]{3,2,1,0:T(8,128)S(1)}, f32[6,3,8,128]{3,2,1,0:T(8,128)S(1)}) custom-call(f32[640,128]{1,0:T(8,128)S(1)} %bitcast.4, f32[2,3,16,8,128]{4,3,2,1,0:T(8,128)S(1)} %get-tuple-element.21.coef_ref.cx_ref, f32[2,3,3,8,128]{4,3,2,1,0:T(8,128)S(1)} %get-tuple-element.22.tree_ref.tx_ref, ...), custom_call_target="tpu_custom_call" | custom-call | flops 4194304 | bytes 524288 | tf_op jit(solution)/shard_map/pallas_call | solution.py:355
  23.1 20.2 %all_to_all.11 = f32[16,24,128]{2,1,0:T(8,128)S(1)} all-to-all(f32[16,24,128]{2,1,0:T(8,128)S(1)} %bitcast.7), channel_id=1, replica_groups=mesh['gx'=16,'gy'=16] {'gy'}, dimensions={0} | all-to-all | bytes 393216 | tf_op jit(solution)/shard_map/all_to_all | solution.py:404
  43.3 1.2 %shard_map.32 = f32[3,2,128,128]{3,2,1,0:T(8,128)} custom-call(f32[384,128]{1,0:T(8,128)S(1)} %bitcast.5, f32[2,3,16,8,128]{4,3,2,1,0:T(8,128)S(1)} %get-tuple-element.27.cy_ref.coef_ref, f32[2,3,3,8,128]{4,3,2,1,0:T(8,128)S(1)} %get-tuple-element.28.ty_ref.tree_ref, f32[6,16,8,128]{3,2,1,0:T(8,128)S(1)} %get-tuple-element.31.q_ref, ...), custom_call_target="tpu_custom_call" | custom-call | flops 4194304 | bytes 524288 | tf_op jit(solution)/shard_map/pallas_call | solution.py:355
Async XLA Ops:
  0.0 1.0 %copy-start = (f32[3,2,128,128]{3,2,1,0:T(8,128)S(1)}, f32[3,2,128,128]{3,2,1,0:T(8,128)}, u32[]{:S(2)}) copy-start(f32[3,2,128,128]{3,2,1,0:T(8,128)} %velocity_ref.3) | copy-start | bytes 1179652
  1.0 6.2 %copy-start.1 = (f32[3,2,128,128]{3,2,1,0:T(8,128)S(1)}, f32[3,2,128,128]{3,2,1,0:T(8,128)}, u32[]{:S(2)}) copy-start(f32[3,2,128,128]{3,2,1,0:T(8,128)} %velocity_ref.3) | copy-start | bytes 1179652
  1.2 4.5 %collective-permute-start = (f32[8,128]{1,0:T(8,128)S(1)}, f32[8,128]{1,0:T(8,128)S(1)}, u32[]{:S(2)}, u32[]{:S(2)}) collective-permute-start(f32[8,128]{1,0:T(8,128)S(1)} %get-tuple-element.19), channel_id=1, source_target_pairs={{0,1},{1,2},{2,3},{3,4},{4,5},{5,6},{6,7},{7,8},{8,9},{9,10},{10,1... | collective-permute-start | bytes 12296 | tf_op jit(solution)/shard_map/ppermute | solution.py:374
  4.2 3.0 %collective-permute-start.1 = (f32[8,128]{1,0:T(8,128)S(1)}, f32[8,128]{1,0:T(8,128)S(1)}, u32[]{:S(2)}, u32[]{:S(2)}) collective-permute-start(f32[8,128]{1,0:T(8,128)S(1)} %get-tuple-element.20), channel_id=1, source_target_pairs={{1,0},{2,1},{3,2},{4,3},{5,4},{6,5},{7,6},{8,7},{9,8},{10,9},{11,1... | collective-permute-start | bytes 12296 | tf_op jit(solution)/shard_map/ppermute | solution.py:375
  4.4 0.9 %copy-start.2 = (f32[2,128,128]{2,1,0:T(8,128)S(1)}, f32[2,128,128]{2,1,0:T(8,128)}, u32[]{:S(2)}) copy-start(f32[2,128,128]{2,1,0:T(8,128)} %diffusion_ref.1) | copy-start | bytes 393220

commit v2 on v1

v2 whole, which is shorter than its diff:
```python
from functools import partial

import jax
import jax.numpy as jnp
from jax import lax
from jax.experimental import pallas as pl
from jax.experimental.pallas import tpu as pltpu
from jax.sharding import PartitionSpec as P


COURANT = 0.25
HALF = 0.5 * COURANT
SEG = 16
PLANES = 2
COMPS = 3
LANES = 128
ROWS_X = 40
ROWS_Y = 24
ROW_G, ROW_EL, ROW_ER, ROW_DHI, ROW_DLO = 0, 2, 4, 6, 8
ROW_JL, ROW_JR, ROW_VLO, ROW_VHI = 10, 16, 22, 28
Y_JL, Y_JR, ROWS_SENT_Y = 6, 12, 18
OWN_A, OWN_B, OWN_Q = 0, 2, 4

f32 = jnp.float32
VMEM = pltpu.VMEM
HBM = pltpu.HBM


def sub_iota():
    return lax.broadcasted_iota(jnp.int32, (8, LANES), 0)


def lane_iota():
    return lax.broadcasted_iota(jnp.int32, (8, LANES), 1)


def ahead(x, count):
    return pltpu.roll(x, 8 - count, 0)


def after(x, count):
    return pltpu.roll(x, count, 0)


def strided(ref, lead, t):
    return ref[lead, pl.ds(t, 8, stride=SEG), :]


def factor(cells, first, coef_ref, tree_ref, head_ref, plane):
    row = sub_iota()
    last = row == 7
    faces = [0.5 * (cells[t] + cells[t + 1]) for t in range(SEG - 1)]
    faces.append(0.5 * (cells[SEG - 1] + ahead(cells[0], 1)))
    leak_l = 1.0 + jnp.where(jnp.logical_and(row == 0, first), 0.5 * cells[0], 0.0)
    g = faces[0]
    leak_r = jnp.ones_like(g)
    for t in range(1, SEG):
        f = faces[t]
        inv = 1.0 / (g + f + leak_r)
        a = g * inv
        b = f * inv
        if t == SEG - 1:
            inv = jnp.where(last, 0.0, inv)
            g = jnp.where(last, g, a * f)
            a = jnp.where(last, 0.0, a)
            b = jnp.where(last, 1.0, b)
            leak_l = leak_l + a * leak_r
            leak_r = b * leak_r
        else:
            g = a * f
            leak_l = leak_l + a * leak_r
            leak_r = 1.0 + b * leak_r
        coef_ref[plane, 0, t] = a
        coef_ref[plane, 1, t] = b
        coef_ref[plane, 2, t] = inv
    for level in range(3):
        count = 1 << level
        g_next = ahead(g, count)
        leak = leak_r + ahead(leak_l, count)
        inv = 1.0 / (g + g_next + leak)
        a = g * inv
        b = g_next * inv
        g = a * g_next
        leak_l = leak_l + a * leak
        leak_r = ahead(leak_r, count) + b * leak
        tree_ref[plane, level, 0] = a
        tree_ref[plane, level, 1] = b
        tree_ref[plane, level, 2] = inv
    for base, value in ((ROW_G, g), (ROW_EL, leak_l), (ROW_ER, leak_r)):
        head_ref[base + plane : base + plane + 1, :] = value[0:1]
    head_ref[ROW_DHI + plane : ROW_DHI + plane + 1, :] = cells[SEG - 1][7:8]
    head_ref[ROW_DLO + plane : ROW_DLO + plane + 1, :] = cells[0][0:1]


def condense(sources, coef_ref, tree_ref, q_ref, qtree_ref, plane, comp):
    k = comp * PLANES + plane
    left = sources[0]
    right = sources[1]
    for t in range(1, SEG):
        q_ref[k, t] = coef_ref[plane, 2, t] * right
        left = left + coef_ref[plane, 0, t] * right
        right = coef_ref[plane, 1, t] * right
        if t < SEG - 1:
            right = right + sources[t + 1]
    for level in range(3):
        count = 1 << level
        j = right + ahead(left, count)
        left = left + tree_ref[plane, level, 0] * j
        right = ahead(right, count) + tree_ref[plane, level, 1] * j
        qtree_ref[k, level] = tree_ref[plane, level, 2] * j
    return left, right


def unfold(low, high, coef_ref, tree_ref, q_ref, qtree_ref, plane, comp, store):
    k = comp * PLANES + plane
    row = sub_iota()

    def mid(level, lo, hi):
        return (
            tree_ref[plane, level, 0] * lo
            + tree_ref[plane, level, 1] * hi
            + qtree_ref[k, level]
        )

    for level in (2, 1, 0):
        count = 1 << level
        between = mid(level, low, high)
        late = (row & count) != 0
        low = jnp.where(late, after(between, count), low)
        high = jnp.where(late, after(high, count), between)
    store(0, low)
    cell = high
    for t in range(SEG - 1, 0, -1):
        cell = (
            coef_ref[plane, 0, t] * low
            + q_ref[k, t]
            + coef_ref[plane, 1, t] * cell
        )
        store(t, cell)


def cyclic(me, half, count):
    return (me + 8 * half + sub_iota()) & (count - 1)


def solve_ring(blocks, me, count):
    halves = []
    for g, leak_l, leak_r, currents in blocks:
        levels = []
        for level in range(3):
            step = 1 << level
            g_next = ahead(g, step)
            leak = leak_r + ahead(leak_l, step)
            inv = 1.0 / (g + g_next + leak)
            a = g * inv
            b = g_next * inv
            g = a * g_next
            leak_l = leak_l + a * leak
            leak_r = ahead(leak_r, step) + b * leak
            levels.append((a, b, inv))
        merged = []
        for left, right in currents:
            terms = []
            for level in range(3):
                step = 1 << level
                a, b, inv = levels[level]
                j = right + ahead(left, step)
                left = left + a * j
                right = ahead(right, step) + b * j
                terms.append(inv * j)
            merged.append((left, right, terms))
        halves.append((g, leak_l, leak_r, levels, merged))
    g, leak_l, leak_r, levels, merged = halves[0]
    g_next, leak_l_next, leak_r_next, _, merged_next = halves[1]
    leak = leak_r + leak_l_next
    inv = 1.0 / (g + g_next + leak)
    a = g * inv
    b = g_next * inv
    total = 1.0 / (leak_l + a * leak + leak_r_next + b * leak)
    ends = []
    for comp in range(COMPS):
        left, right, terms = merged[comp]
        left_next, right_next, _ = merged_next[comp]
        j = right + left_next
        first = (left + a * j + right_next + b * j) * total
        high = (a + b) * first + inv * j
        for level in (2, 1, 0):
            high = levels[level][0] * first + levels[level][1] * high + terms[level]
        ends.append((first, jnp.where(me == count - 1, 0.0, high)))
    return ends


def solve_x(ring_ref, me, count, plane):
    row = sub_iota()

    def take(which, half):
        return ring_ref[pl.ds(8 * half * ROWS_X + which + plane, 8, stride=ROWS_X), :]

    def both(which):
        return take(which, 0), take(which, 1)

    def before(pair, half):
        return jnp.where(row == 0, after(pair[1 - half], 1), after(pair[half], 1))

    def beyond(pair, half):
        return jnp.where(row == 7, ahead(pair[1 - half], 1), ahead(pair[half], 1))

    first_faces = both(ROW_DLO)
    low_cells = [both(ROW_VLO + comp * PLANES) for comp in range(COMPS)]
    high_cells = [both(ROW_VHI + comp * PLANES) for comp in range(COMPS)]
    blocks = []
    own = None
    for half in (0, 1):
        place = cyclic(me, half, count)
        wall = place == count - 1
        g = take(ROW_G, half)
        leak_l = take(ROW_EL, half)
        leak_r = take(ROW_ER, half)
        f = 0.5 * (take(ROW_DHI, half) + jnp.where(wall, 0.0, beyond(first_faces, half)))
        inv = 1.0 / (g + f + leak_r)
        a = g * inv
        b = f * inv
        through = a * f
        leak_l = leak_l + a * leak_r
        leak_l = jnp.where(wall, leak_l + through, leak_l)
        up_lo = jnp.where(place == 0, 0.0, HALF * low_cells[0][half])
        up_hi = jnp.where(wall, 0.0, HALF * high_cells[0][half])
        b_cut = jnp.where(wall, 0.0, b)
        currents = []
        terms = []
        for comp in range(COMPS):
            left = take(ROW_JL + comp * PLANES, half)
            right = take(ROW_JR + comp * PLANES, half)
            left = left + up_lo * before(high_cells[comp], half)
            right = right - up_hi * beyond(low_cells[comp], half)
            terms.append(inv * right)
            currents.append((left + a * right, b_cut * right))
        if half == 0:
            own = (a, b, terms)
        blocks.append((jnp.where(wall, 0.0, through), leak_l, b_cut * leak_r, currents))
    ends = solve_ring(blocks, me, count)
    a, b, terms = own
    return [
        (first, a * first + b * high + terms[comp]) for comp, (first, high) in enumerate(ends)
    ]


def solve_y(ring_ref, own_ref, me, count, plane):
    def take(which, half):
        return ring_ref[pl.ds(8 * half * ROWS_Y + which + plane, 8, stride=ROWS_Y), :]

    def own(which):
        return own_ref[which + plane : which + plane + 1, :]

    blocks = [
        (
            take(ROW_G, half),
            take(ROW_EL, half),
            take(ROW_ER, half),
            [
                (take(Y_JL + comp * PLANES, half), take(Y_JR + comp * PLANES, half))
                for comp in range(COMPS)
            ],
        )
        for half in (0, 1)
    ]
    ends = solve_ring(blocks, me, count)
    return [
        (first, own(OWN_A) * first + own(OWN_B) * high + own(OWN_Q + comp * PLANES))
        for comp, (first, high) in enumerate(ends)
    ]


def edges_kernel(velocity_ref, diffusion_ref, low_ref, high_ref, v_ref, d_ref, turn_ref, sem):
    copies = [
        pltpu.make_async_copy(velocity_ref, v_ref, sem.at[0]),
        pltpu.make_async_copy(diffusion_ref, d_ref, sem.at[1]),
    ]
    for copy in copies:
        copy.start()
    for copy in copies:
        copy.wait()
    for k in range(COMPS * PLANES + PLANES):
        if k < COMPS * PLANES:
            comp, plane = divmod(k, PLANES)
            turned = jnp.transpose(v_ref[comp, plane])
        else:
            turned = jnp.transpose(d_ref[k - 6])
            turn_ref[k - 6] = turned
        low_ref[k : k + 1, :] = turned[0:1]
        high_ref[k : k + 1, :] = turned[LANES - 1 : LANES]


def matrix_kernel(diffusion_ref, turn_ref, cx_ref, tx_ref, hx_ref, cy_ref, ty_ref, hy_ref):
    first_x = lax.axis_index("gx") == 0
    first_y = lax.axis_index("gy") == 0
    for plane in range(PLANES):
        cells = [strided(diffusion_ref, plane, t) for t in range(SEG)]
        factor(cells, first_x, cx_ref, tx_ref, hx_ref, plane)
        cells = [strided(turn_ref, plane, t) for t in range(SEG)]
        factor(cells, first_y, cy_ref, ty_ref, hy_ref, plane)
    for ref in (hx_ref, hy_ref):
        ref[10:16, :] = jnp.zeros((6, LANES), f32)


def source_kernel(count, velocity_ref, from_low_ref, from_high_ref, coef_ref, tree_ref, head_ref,
                  out_ref, q_ref, qtree_ref, edge_ref, halo_ref, page_ref):
    me_y = lax.axis_index("gy")
    count_y = lax.axis_size("gy")
    row = sub_iota()
    lane = lane_iota()
    low = jnp.where(me_y == 0, 0.0, from_low_ref[...])
    high = jnp.where(me_y == count_y - 1, 0.0, from_high_ref[...])
    edge_ref[0:8, :] = low
    edge_ref[8:16, :] = high
    edge_ref[16:, :] = jnp.zeros((LANES - 16, LANES), f32)
    halo_ref[...] = jnp.transpose(edge_ref[...])
    page_ref[0:16, :] = head_ref[...]
    page_ref[32:, :] = jnp.zeros((ROWS_X - 32, LANES), f32)
    for plane in range(PLANES):
        cells = [
            [velocity_ref[comp, plane, pl.ds(t, 8, stride=SEG), :] for t in range(SEG)]
            for comp in range(COMPS)
        ]
        halos = [halo_ref[pl.ds(t, 8, stride=SEG), :] for t in range(SEG)]
        for comp in range(COMPS):
            k = comp * PLANES + plane
            own = cells[comp]
            sources = []
            for t in range(SEG):
                if t < SEG - 1:
                    fore = own[t + 1]
                else:
                    fore = jnp.where(row == 7, 0.0, ahead(own[0], 1))
                if t > 0:
                    back = own[t - 1]
                else:
                    back = jnp.where(row == 0, 0.0, after(own[SEG - 1], 1))
                lo = jnp.broadcast_to(halos[t][:, k : k + 1], (8, LANES))
                hi = jnp.broadcast_to(halos[t][:, 8 + k : 9 + k], (8, LANES))
                right = jnp.where(lane == LANES - 1, hi, pltpu.roll(own[t], LANES - 1, 1))
                left = jnp.where(lane == 0, lo, pltpu.roll(own[t], 1, 1))
                sources.append(
                    own[t]
                    - HALF * (cells[0][t] * (fore - back) + cells[1][t] * (right - left))
                )
            left, right = condense(sources, coef_ref, tree_ref, q_ref, qtree_ref, plane, comp)
            page_ref[ROW_JL + k : ROW_JL + k + 1, :] = left[0:1]
            page_ref[ROW_JR + k : ROW_JR + k + 1, :] = right[0:1]
            page_ref[ROW_VLO + k : ROW_VLO + k + 1, :] = own[0][0:1]
            page_ref[ROW_VHI + k : ROW_VHI + k + 1, :] = own[SEG - 1][7:8]
    page = page_ref[...]
    for i in range(count):
        out_ref[i] = page


def middle_kernel(count_x, count_y, got_ref, from_high_ref, cx_ref, tx_ref, qx_ref, qtx_ref, cy_ref,
                  ty_ref, hy_ref, out_ref, q_ref, qtree_ref, own_ref, ring_ref, plane_ref, turn_ref):
    me = lax.axis_index("gx")
    wall = lax.axis_index("gy") == count_y - 1
    for i in range(count_x):
        slot = (i - me + count_x) & (count_x - 1)
        ring_ref[pl.ds(pl.multiple_of(slot * ROWS_X, 8), ROWS_X), :] = got_ref[i]
    own_ref[10:16, :] = jnp.zeros((6, LANES), f32)
    values = {}
    for plane in range(PLANES):

        def head(which):
            return hy_ref[which + plane : which + plane + 1, :]

        g = head(ROW_G)
        leak_r = head(ROW_ER)
        beyond = from_high_ref[6 + plane : 7 + plane, :]
        f = 0.5 * (head(ROW_DHI) + jnp.where(wall, 0.0, beyond))
        inv = 1.0 / (g + f + leak_r)
        a = g * inv
        b = f * inv
        through = a * f
        b_cut = jnp.where(wall, 0.0, b)
        own_ref[OWN_A + plane : OWN_A + plane + 1, :] = a
        own_ref[OWN_B + plane : OWN_B + plane + 1, :] = b
        values[ROW_G + plane] = jnp.where(wall, 0.0, through)
        leak_l = head(ROW_EL) + a * leak_r
        values[ROW_EL + plane] = jnp.where(wall, leak_l + through, leak_l)
        values[ROW_ER + plane] = b_cut * leak_r
        ends = solve_x(ring_ref, me, count_x, plane)
        for comp in range(COMPS):
            k = comp * PLANES + plane
            low, high = ends[comp]

            def store(t, value):
                plane_ref[k, pl.ds(t, 8, stride=SEG), :] = value

            unfold(low, high, cx_ref, tx_ref, qx_ref, qtx_ref, plane, comp, store)
            turn_ref[k] = jnp.transpose(plane_ref[k])
            sources = [strided(turn_ref, k, t) for t in range(SEG)]
            left, right = condense(sources, cy_ref, ty_ref, q_ref, qtree_ref, plane, comp)
            right = right[0:1]
            own_ref[OWN_Q + k : OWN_Q + k + 1, :] = inv * right
            values[Y_JL + k] = left[0:1] + a * right
            values[Y_JR + k] = b_cut * right
    for pair in range(ROWS_SENT_Y // 2):
        rows = jnp.concatenate([values[2 * pair], values[2 * pair + 1]], 0)
        for i in range(count_y):
            out_ref[i, pair] = rows


def final_kernel(count, got_ref, own_ref, coef_ref, tree_ref, q_ref, qtree_ref, out_ref, ring_ref,
                 plane_ref, turn_ref, sem):
    me = lax.axis_index("gy")
    for i in range(count):
        slot = (i - me + count) & (count - 1)
        base = slot * ROWS_Y
        for pair in range(ROWS_SENT_Y // 2):
            ring_ref[pl.ds(base + 2 * pair, 2), :] = got_ref[i, pair]
    copies = []
    for plane in range(PLANES):
        ends = solve_y(ring_ref, own_ref, me, count, plane)
        for comp in range(COMPS):
            k = comp * PLANES + plane
            low, high = ends[comp]

            def store(t, value):
                plane_ref[k, pl.ds(t, 8, stride=SEG), :] = value

            unfold(low, high, coef_ref, tree_ref, q_ref, qtree_ref, plane, comp, store)
            turn_ref[k] = jnp.transpose(plane_ref[k])
            copy = pltpu.make_async_copy(turn_ref.at[k], out_ref.at[comp, plane], sem.at[k])
            copy.start()
            copies.append(copy)
    for copy in copies:
        copy.wait()


def shape(*dims):
    return jax.ShapeDtypeStruct(dims, f32)


def call(kernel, ins, outs, scratch, cost, *args):
    return pl.pallas_call(
        kernel,
        out_shape=tuple(o for o, _ in outs),
        in_specs=[pl.BlockSpec(memory_space=m) for m in ins],
        out_specs=tuple(pl.BlockSpec(memory_space=m) for _, m in outs),
        scratch_shapes=scratch,
        cost_estimate=pl.CostEstimate(flops=cost, bytes_accessed=1 << 19, transcendentals=0),
        compiler_params=pltpu.CompilerParams(vmem_limit_bytes=8 << 20),
    )(*args)


def local(velocity, diffusion):
    count_x = lax.axis_size("gx")
    count_y = lax.axis_size("gy")
    tile = (8, LANES)
    n = COMPS * PLANES
    low, high, cells, diff, turned = call(
        edges_kernel,
        (HBM, HBM),
        [
            (shape(*tile), VMEM),
            (shape(*tile), VMEM),
            (shape(COMPS, PLANES, LANES, LANES), VMEM),
            (shape(PLANES, LANES, LANES), VMEM),
            (shape(PLANES, LANES, LANES), VMEM),
        ],
        [pltpu.SemaphoreType.DMA((2,))],
        1 << 17,
        pltpu.with_memory_space_constraint(velocity, HBM),
        pltpu.with_memory_space_constraint(diffusion, HBM),
    )
    from_low = lax.ppermute(high, "gy", [(i, (i + 1) % count_y) for i in range(count_y)])
    from_high = lax.ppermute(low, "gy", [((i + 1) % count_y, i) for i in range(count_y)])
    coef = (shape(PLANES, 3, SEG, *tile), VMEM)
    tree = (shape(PLANES, 3, 3, *tile), VMEM)
    head = (shape(16, LANES), VMEM)
    q_all = (shape(n, SEG, *tile), VMEM)
    q_tree = (shape(n, 3, *tile), VMEM)
    block = VMEM((n, LANES, LANES), f32)
    cx, tx, hx, cy, ty, hy = call(
        matrix_kernel, (VMEM,) * 2, [coef, tree, head] * 2, [], 1 << 21, diff, turned
    )
    sent, qx, qtx = call(
        partial(source_kernel, count_x),
        (VMEM,) * 6,
        [(shape(count_x, ROWS_X, LANES), VMEM), q_all, q_tree],
        [VMEM((LANES, LANES), f32), VMEM((LANES, LANES), f32), VMEM((ROWS_X, LANES), f32)],
        1 << 22,
        cells, from_low, from_high, cx, tx, hx,
    )
    got = lax.all_to_all(sent, "gx", 0, 0)
    sent, qy, qty, own = call(
        partial(middle_kernel, count_x, count_y),
        (VMEM,) * 9,
        [(shape(count_y, ROWS_SENT_Y // 2, 2, LANES), VMEM), q_all, q_tree, head],
        [VMEM((count_x * ROWS_X, LANES), f32), block, block],
        1 << 22,
        got, from_high, cx, tx, qx, qtx, cy, ty, hy,
    )
    got = lax.all_to_all(sent, "gy", 0, 0)
    (result,) = call(
        partial(final_kernel, count_y),
        (VMEM,) * 6,
        [(shape(COMPS, PLANES, LANES, LANES), HBM)],
        [
            VMEM((count_y * ROWS_Y, LANES), f32),
            block,
            block,
            pltpu.SemaphoreType.DMA((n,)),
        ],
        1 << 22,
        got, own, cy, ty, qy, qty,
    )
    return result


def solution(mesh):
    in_specs = (P(None, None, "gx", "gy"), P(None, "gx", "gy"))
    out_specs = P(None, None, "gx", "gy")
    return jax.shard_map(local, mesh=mesh, in_specs=in_specs, out_specs=out_specs, check_vma=False)
```

time: 44.7 us -> 43.7 us (0.978)
  local copies, waits for them, and re-layouts: 1.9 us -> 0 us
  Pallas kernels: 3.04 us -> 4.07 us
  blocking collectives: 34.7 us -> 33.7 us
  waiting for transfers between devices: 1.6 us -> 2.57 us
    unnamed x6 -> x0, local copies, waits for them, and re-layouts: 1.9 us -> none
    pallas_call x5, Pallas kernels: 3.04 us -> 4.07 us  [call(): pl.pallas_call(kernel, out_shape=tuple((o for o, _ in outs)), in_specs=[p...]
    all_to_all x2, blocking collectives: 34.7 us -> 33.7 us  [the longest x1 19.2 us: local(): got = lax.all_to_all(sent, 'gy', 0, 0)]
    ppermute x1, waiting for transfers between devices: 1.6 us -> 2.19 us  [local(): lax.ppermute(low, 'gy', [((i + 1) % count_y, i) for i in range(count_y)])]
  transfers between devices with their start and end apart: 2 -> 2, of which waited for: 1 -> 2; matrix products, arithmetic and copies ran while one was open for 0% -> 0% of each run, Pallas kernels for 1% -> 1%
where the time goes in v2:
time: 43.7 us; the launch traced here: 43.6 us
  blocking collectives  33.7 us (77%)
  Pallas kernels  4.07 us (9%)
  starting transfers between devices  3.24 us (7%)
  waiting for transfers between devices  2.57 us (6%)
    all_to_all x1, blocking collectives, local(): got = lax.all_to_all(sent, 'gy', 0, 0)  19.2 us
    all_to_all x1, blocking collectives, local(): got = lax.all_to_all(sent, 'gx', 0, 0)  14.4 us
    pallas_call x5, Pallas kernels, call(): pl.pallas_call(kernel, out_shape=tuple((o for o, _ in outs)), in_specs=[p...  4.07 us
    ppermute x1, starting transfers between devices, local(): lax.ppermute(high, 'gy', [(i, (i + 1) % count_y) for i in range(count_y)])  3.03 us
    ppermute x1, waiting for transfers between devices, local(): lax.ppermute(low, 'gy', [((i + 1) % count_y, i) for i in range(count_y)])  2.19 us
  transfers between devices with their start and end apart: 2, of which 2 were waited for; matrix products, arithmetic and copies ran while one was open for 0% of the time, Pallas kernels for 1%

profile of v2, /device:TPU:1, one launch (start us, length us, event | category | flops | bytes accessed | tf_op | source)
XLA Modules:
  0.0 43.6 jit_solution(15564271868213039362)
XLA Ops:
  0.0 1.2 %shard_map.28 = (f32[8,128]{1,0:T(8,128)S(1)}, f32[8,128]{1,0:T(8,128)S(1)}, f32[3,2,128,128]{3,2,1,0:T(8,128)S(1)}, f32[2,128,128]{2,1,0:T(8,128)S(1)}, f32[2,128,128]{2,1,0:T(8,128)S(1)}) custom-call(f32[3,2,128,128]{3,2,1,0:T(8,128)} %velocity_ref.1, f32[2,128,128]{2,1,0:T(8,128)} %diffusion_ref.1), custom_call_target="tpu_custom_call" | custom-call | flops 131072 | bytes 524288 | tf_op jit(solution)/shard_map/pallas_call | solution.py:440
  1.2 3.0 %collective-permute-start = (f32[8,128]{1,0:T(8,128)S(1)}, f32[8,128]{1,0:T(8,128)S(1)}, u32[]{:S(2)}, u32[]{:S(2)}) collective-permute-start(f32[8,128]{1,0:T(8,128)S(1)} %get-tuple-element.24), channel_id=1, source_target_pairs={{0,1},{1,2},{2,3},{3,4},{4,5},{5,6},{6,7},{7,8},{8,9},{9,10},{10,1... | collective-permute-start | bytes 12296 | tf_op jit(solution)/shard_map/ppermute | solution.py:471
  4.3 0.2 collective-permute-start.1
  4.5 0.2 shard_map.29
  4.7 0.4 collective-permute-done.from_low_ref
  5.1 2.2 %collective-permute-done.1.from_high_ref = f32[8,128]{1,0:T(8,128)S(1)} collective-permute-done((f32[8,128]{1,0:T(8,128)S(1)}, f32[8,128]{1,0:T(8,128)S(1)}, u32[]{:S(2)}, u32[]{:S(2)}) %collective-permute-start.1) | collective-permute-done | bytes 4128 | tf_op jit(solution)/shard_map/ppermute | solution.py:472
  7.3 0.9 %shard_map.30 = (f32[16,40,128]{2,1,0:T(8,128)S(1)}, f32[6,16,8,128]{3,2,1,0:T(8,128)S(1)}, f32[6,3,8,128]{3,2,1,0:T(8,128)S(1)}) custom-call(f32[3,2,128,128]{3,2,1,0:T(8,128)S(1)} %get-tuple-element.23.velocity_ref, f32[8,128]{1,0:T(8,128)S(1)} %collective-permute-done.from_low_ref, f32[8,128]{1,0:T(8,128)S(1)} %collective-permute-done.1.from_high_ref, ...), custom_call_target="tpu_custom_call" | custom-call | flops 4194304 | bytes 524288 | tf_op jit(solution)/shard_map/pallas_call | solution.py:440
  8.2 14.4 %all_to_all.10.got_ref = f32[16,40,128]{2,1,0:T(8,128)S(1)} all-to-all(f32[16,40,128]{2,1,0:T(8,128)S(1)} %get-tuple-element.31), channel_id=1, replica_groups=mesh['gx'=16,'gy'=16] {'gx'}, dimensions={0} | all-to-all | bytes 655360 | tf_op jit(solution)/shard_map/all_to_all | solution.py:490
  22.6 0.6 %shard_map.31 = (f32[16,9,2,128]{3,2,1,0:T(2,128)S(1)}, f32[6,16,8,128]{3,2,1,0:T(8,128)S(1)}, f32[6,3,8,128]{3,2,1,0:T(8,128)S(1)}, f32[16,128]{1,0:T(8,128)S(1)}) custom-call(f32[16,40,128]{2,1,0:T(8,128)S(1)} %all_to_all.10.got_ref, f32[8,128]{1,0:T(8,128)S(1)} %collective-permute-done.1.from_high_ref, ...), custom_call_target="tpu_custom_call" | custom-call | flops 4194304 | bytes 524288 | tf_op jit(solution)/shard_map/pallas_call | solution.py:440
  23.3 19.2 %all_to_all.11.got_ref = f32[16,9,2,128]{3,2,1,0:T(2,128)S(1)} all-to-all(f32[16,9,2,128]{3,2,1,0:T(2,128)S(1)} %get-tuple-element.37), channel_id=1, replica_groups=mesh['gx'=16,'gy'=16] {'gy'}, dimensions={0} | all-to-all | bytes 294912 | tf_op jit(solution)/shard_map/all_to_all | solution.py:499
  42.5 1.1 %shard_map.32 = f32[3,2,128,128]{3,2,1,0:T(8,128)} custom-call(f32[16,9,2,128]{3,2,1,0:T(2,128)S(1)} %all_to_all.11.got_ref, f32[16,128]{1,0:T(8,128)S(1)} %get-tuple-element.38.own_ref, f32[2,3,16,8,128]{4,3,2,1,0:T(8,128)S(1)} %get-tuple-element.34.cy_ref.coef_ref, f32[2,3,3,8,128]{4,3,2,1,0:T(8,128)S(1)} %get-tuple-element.35.ty_ref.tree_ref, ...), custom_call_target="tpu_custom_call" | custom-call | flops 4194304 | bytes 524288 | tf_op jit(solution)/shard_map/pallas_call | solution.py:440
Async XLA Ops:
  1.2 3.9 %collective-permute-start = (f32[8,128]{1,0:T(8,128)S(1)}, f32[8,128]{1,0:T(8,128)S(1)}, u32[]{:S(2)}, u32[]{:S(2)}) collective-permute-start(f32[8,128]{1,0:T(8,128)S(1)} %get-tuple-element.24), channel_id=1, source_target_pairs={{0,1},{1,2},{2,3},{3,4},{4,5},{5,6},{6,7},{7,8},{8,9},{9,10},{10,1... | collective-permute-start | bytes 12296 | tf_op jit(solution)/shard_map/ppermute | solution.py:471
  4.3 3.0 %collective-permute-start.1 = (f32[8,128]{1,0:T(8,128)S(1)}, f32[8,128]{1,0:T(8,128)S(1)}, u32[]{:S(2)}, u32[]{:S(2)}) collective-permute-start(f32[8,128]{1,0:T(8,128)S(1)} %get-tuple-element.25), channel_id=1, source_target_pairs={{1,0},{2,1},{3,2},{4,3},{5,4},{6,5},{7,6},{8,7},{9,8},{10,9},{11,1... | collective-permute-start | bytes 12296 | tf_op jit(solution)/shard_map/ppermute | solution.py:472

commit v3 on v2

--- a/solution.py
+++ b/solution.py
@@ -16,8 +16,10 @@
 LANES = 128
 ROWS_X = 40
 ROWS_Y = 24
-ROW_G, ROW_EL, ROW_ER, ROW_DHI, ROW_DLO = 0, 2, 4, 6, 8
-ROW_JL, ROW_JR, ROW_VLO, ROW_VHI = 10, 16, 22, 28
+ROW_G, ROW_EL, ROW_ER, ROW_DHI, ROW_VLO, ROW_DLO = 0, 2, 4, 6, 8, 14
+ROW_JL, ROW_JR, ROW_VHI = 16, 24, 30
+TILE_X = 2
+SENT_X = [i for i in range(0, 36, TILE_X) if i != 22]
 Y_JL, Y_JR, ROWS_SENT_Y = 6, 12, 18
 OWN_A, OWN_B, OWN_Q = 0, 2, 4
 
@@ -86,6 +88,8 @@
         tree_ref[plane, level, 0] = a
         tree_ref[plane, level, 1] = b
         tree_ref[plane, level, 2] = inv
+    if head_ref is None:
+        return
     for base, value in ((ROW_G, g), (ROW_EL, leak_l), (ROW_ER, leak_r)):
         head_ref[base + plane : base + plane + 1, :] = value[0:1]
     head_ref[ROW_DHI + plane : ROW_DHI + plane + 1, :] = cells[SEG - 1][7:8]
@@ -291,38 +295,39 @@
         high_ref[k : k + 1, :] = turned[LANES - 1 : LANES]
 
 
-def matrix_kernel(diffusion_ref, turn_ref, cx_ref, tx_ref, hx_ref, cy_ref, ty_ref, hy_ref):
+def matrix_kernel(diffusion_ref, turn_ref, low_ref, high_ref, cx_ref, tx_ref, hx_ref, cy_ref, ty_ref,
+                  hy_ref, cp_ref, tp_ref, vp_ref, edge_ref, pack_ref):
     first_x = lax.axis_index("gx") == 0
     first_y = lax.axis_index("gy") == 0
+    edge_ref[...] = jnp.zeros((2, LANES, LANES), f32)
+    for i, base in enumerate((2, 6)):
+        for k in range(COMPS * PLANES):
+            line = base + k % PLANES
+            edge_ref[i, k : k + 1, :] = low_ref[line : line + 1, :]
+            edge_ref[i, 8 + k : 9 + k, :] = high_ref[line : line + 1, :]
+    vp_ref[...] = jnp.transpose(edge_ref[0])
+    pack_ref[0] = jnp.transpose(edge_ref[1])
     for plane in range(PLANES):
         cells = [strided(diffusion_ref, plane, t) for t in range(SEG)]
         factor(cells, first_x, cx_ref, tx_ref, hx_ref, plane)
         cells = [strided(turn_ref, plane, t) for t in range(SEG)]
         factor(cells, first_y, cy_ref, ty_ref, hy_ref, plane)
+    cells = [strided(pack_ref, 0, t) for t in range(SEG)]
+    factor(cells, first_x, cp_ref, tp_ref, None, 0)
     for ref in (hx_ref, hy_ref):
-        ref[10:16, :] = jnp.zeros((6, LANES), f32)
-
-
-def source_kernel(count, velocity_ref, from_low_ref, from_high_ref, coef_ref, tree_ref, head_ref,
-                  out_ref, q_ref, qtree_ref, edge_ref, halo_ref, page_ref):
-    me_y = lax.axis_index("gy")
-    count_y = lax.axis_size("gy")
+        ref[ROW_VLO : ROW_VLO + 6, :] = jnp.zeros((6, LANES), f32)
+
+
+def source_kernel(velocity_ref, coef_ref, tree_ref, head_ref, page_ref, q_ref, qtree_ref):
     row = sub_iota()
     lane = lane_iota()
-    low = jnp.where(me_y == 0, 0.0, from_low_ref[...])
-    high = jnp.where(me_y == count_y - 1, 0.0, from_high_ref[...])
-    edge_ref[0:8, :] = low
-    edge_ref[8:16, :] = high
-    edge_ref[16:, :] = jnp.zeros((LANES - 16, LANES), f32)
-    halo_ref[...] = jnp.transpose(edge_ref[...])
     page_ref[0:16, :] = head_ref[...]
-    page_ref[32:, :] = jnp.zeros((ROWS_X - 32, LANES), f32)
+    page_ref[16:, :] = jnp.zeros((ROWS_X - 16, LANES), f32)
     for plane in range(PLANES):
         cells = [
             [velocity_ref[comp, plane, pl.ds(t, 8, stride=SEG), :] for t in range(SEG)]
             for comp in range(COMPS)
         ]
-        halos = [halo_ref[pl.ds(t, 8, stride=SEG), :] for t in range(SEG)]
         for comp in range(COMPS):
             k = comp * PLANES + plane
             own = cells[comp]
@@ -336,10 +341,8 @@
                     back = own[t - 1]
                 else:
                     back = jnp.where(row == 0, 0.0, after(own[SEG - 1], 1))
-                lo = jnp.broadcast_to(halos[t][:, k : k + 1], (8, LANES))
-                hi = jnp.broadcast_to(halos[t][:, 8 + k : 9 + k], (8, LANES))
-                right = jnp.where(lane == LANES - 1, hi, pltpu.roll(own[t], LANES - 1, 1))
-                left = jnp.where(lane == 0, lo, pltpu.roll(own[t], 1, 1))
+                right = jnp.where(lane == LANES - 1, 0.0, pltpu.roll(own[t], LANES - 1, 1))
+                left = jnp.where(lane == 0, 0.0, pltpu.roll(own[t], 1, 1))
                 sources.append(
                     own[t]
                     - HALF * (cells[0][t] * (fore - back) + cells[1][t] * (right - left))
@@ -349,18 +352,55 @@
             page_ref[ROW_JR + k : ROW_JR + k + 1, :] = right[0:1]
             page_ref[ROW_VLO + k : ROW_VLO + k + 1, :] = own[0][0:1]
             page_ref[ROW_VHI + k : ROW_VHI + k + 1, :] = own[SEG - 1][7:8]
-    page = page_ref[...]
-    for i in range(count):
-        out_ref[i] = page
+
+
+def halo_kernel(count, from_low_ref, from_high_ref, vp_ref, coef_ref, tree_ref, page_ref, out_ref,
+                q_ref, qtree_ref, edge_ref, halo_ref):
+    me_y = lax.axis_index("gy")
+    count_y = lax.axis_size("gy")
+    row = sub_iota()
+    lane = lane_iota()
+    edge_ref[0:8, :] = jnp.where(me_y == 0, 0.0, HALF * from_low_ref[...])
+    edge_ref[8:16, :] = jnp.where(me_y == count_y - 1, 0.0, -HALF * from_high_ref[...])
+    edge_ref[16:, :] = jnp.zeros((LANES - 16, LANES), f32)
+    halo_ref[...] = jnp.transpose(edge_ref[...])
+    sources = [
+        vp_ref[pl.ds(t, 8, stride=SEG), :] * halo_ref[pl.ds(t, 8, stride=SEG), :]
+        for t in range(SEG)
+    ]
+    ends = condense(sources, coef_ref, tree_ref, q_ref, qtree_ref, 0, 0)
+    page = [page_ref[8 * i : 8 * i + 8, :] for i in range(ROWS_X // 8)]
+    for base, value in zip((ROW_JL, ROW_JR), ends):
+        value = jnp.broadcast_to(value[0:1], (8, LANES))
+        low = jnp.sum(jnp.where(lane == row, value, 0.0), axis=1, keepdims=True)
+        high = jnp.sum(jnp.where(lane == row + 8, value, 0.0), axis=1, keepdims=True)
+        extra = jnp.where(lane == 0, low, jnp.where(lane == LANES - 1, high, 0.0))
+        page[base // 8] = page[base // 8] + extra
+    for i, rows in enumerate(page):
+        edge_ref[8 * i : 8 * i + 8, :] = rows
+    for j, start in enumerate(SENT_X):
+        rows = edge_ref[start : start + TILE_X, :]
+        for i in range(count):
+            out_ref[i, j] = rows
 
 
 def middle_kernel(count_x, count_y, got_ref, from_high_ref, cx_ref, tx_ref, qx_ref, qtx_ref, cy_ref,
-                  ty_ref, hy_ref, out_ref, q_ref, qtree_ref, own_ref, ring_ref, plane_ref, turn_ref):
+                  ty_ref, hy_ref, cp_ref, tp_ref, qp_ref, qtp_ref, out_ref, q_ref, qtree_ref, own_ref,
+                  ring_ref, plane_ref, turn_ref, pack_ref, extra_ref):
     me = lax.axis_index("gx")
+
+    def store_pack(t, value):
+        pack_ref[pl.ds(t, 8, stride=SEG), :] = value
+
+    nothing = jnp.zeros((8, LANES), f32)
+    unfold(nothing, nothing, cp_ref, tp_ref, qp_ref, qtp_ref, 0, 0, store_pack)
+    extra_ref[...] = jnp.transpose(pack_ref[...])
     wall = lax.axis_index("gy") == count_y - 1
     for i in range(count_x):
         slot = (i - me + count_x) & (count_x - 1)
-        ring_ref[pl.ds(pl.multiple_of(slot * ROWS_X, 8), ROWS_X), :] = got_ref[i]
+        base = slot * ROWS_X
+        for j, start in enumerate(SENT_X):
+            ring_ref[pl.ds(base + start, TILE_X), :] = got_ref[i, j]
     own_ref[10:16, :] = jnp.zeros((6, LANES), f32)
     values = {}
     for plane in range(PLANES):
@@ -392,7 +432,10 @@
                 plane_ref[k, pl.ds(t, 8, stride=SEG), :] = value
 
             unfold(low, high, cx_ref, tx_ref, qx_ref, qtx_ref, plane, comp, store)
-            turn_ref[k] = jnp.transpose(plane_ref[k])
+            turned = jnp.transpose(plane_ref[k])
+            turn_ref[k] = turned
+            turn_ref[k, 0:1, :] = turned[0:1] + extra_ref[k : k + 1, :]
+            turn_ref[k, LANES - 1 :, :] = turned[LANES - 1 :] + extra_ref[8 + k : 9 + k, :]
             sources = [strided(turn_ref, k, t) for t in range(SEG)]
             left, right = condense(sources, cy_ref, ty_ref, q_ref, qtree_ref, plane, comp)
             right = right[0:1]
@@ -476,25 +519,46 @@
     q_all = (shape(n, SEG, *tile), VMEM)
     q_tree = (shape(n, 3, *tile), VMEM)
     block = VMEM((n, LANES, LANES), f32)
-    cx, tx, hx, cy, ty, hy = call(
-        matrix_kernel, (VMEM,) * 2, [coef, tree, head] * 2, [], 1 << 21, diff, turned
+    square = VMEM((LANES, LANES), f32)
+    pair = VMEM((PLANES, LANES, LANES), f32)
+    coef_pack = (shape(1, 3, SEG, *tile), VMEM)
+    tree_pack = (shape(1, 3, 3, *tile), VMEM)
+    cx, tx, hx, cy, ty, hy, cp, tp, vp = call(
+        matrix_kernel,
+        (VMEM,) * 4,
+        [coef, tree, head] * 2 + [coef_pack, tree_pack, (shape(LANES, LANES), VMEM)],
+        [pair, pair],
+        1 << 21,
+        diff, turned, low, high,
     )
-    sent, qx, qtx = call(
-        partial(source_kernel, count_x),
+    page, qx, qtx = call(
+        source_kernel,
+        (VMEM,) * 4,
+        [(shape(ROWS_X, LANES), VMEM), q_all, q_tree],
+        [],
+        1 << 22,
+        cells, cx, tx, hx,
+    )
+    sent, qp, qtp = call(
+        partial(halo_kernel, count_x),
         (VMEM,) * 6,
-        [(shape(count_x, ROWS_X, LANES), VMEM), q_all, q_tree],
-        [VMEM((LANES, LANES), f32), VMEM((LANES, LANES), f32), VMEM((ROWS_X, LANES), f32)],
-        1 << 22,
-        cells, from_low, from_high, cx, tx, hx,
+        [
+            (shape(count_x, len(SENT_X), TILE_X, LANES), VMEM),
+            (shape(1, SEG, *tile), VMEM),
+            (shape(1, 3, *tile), VMEM),
+        ],
+        [square, square],
+        1 << 18,
+        from_low, from_high, vp, cp, tp, page,
     )
     got = lax.all_to_all(sent, "gx", 0, 0)
     sent, qy, qty, own = call(
         partial(middle_kernel, count_x, count_y),
-        (VMEM,) * 9,
+        (VMEM,) * 13,
         [(shape(count_y, ROWS_SENT_Y // 2, 2, LANES), VMEM), q_all, q_tree, head],
-        [VMEM((count_x * ROWS_X, LANES), f32), block, block],
+        [VMEM((count_x * ROWS_X, LANES), f32), block, block, square, square],
         1 << 22,
-        got, from_high, cx, tx, qx, qtx, cy, ty, hy,
+        got, from_high, cx, tx, qx, qtx, cy, ty, hy, cp, tp, qp, qtp,
     )
     got = lax.all_to_all(sent, "gy", 0, 0)
     (result,) = call(

time: 43.7 us -> 42.7 us (0.977)
  blocking collectives: 33.7 us -> 33.2 us
  waiting for transfers between devices: 2.57 us -> 2.1 us
    pallas_call x5 -> x6, Pallas kernels: 4.07 us -> 3.95 us  [call(): pl.pallas_call(kernel, out_shape=tuple((o for o, _ in outs)), in_specs=[p...]
  transfers between devices with their start and end apart: 2 -> 2, of which waited for: 2 -> 1; matrix products, arithmetic and copies ran while one was open for 0% -> 0% of each run, Pallas kernels for 1% -> 2%
where the time goes in v3:
time: 42.7 us; the launch traced here: 42.5 us
  blocking collectives  33.2 us (78%)
  Pallas kernels  3.95 us (9%)
  starting transfers between devices  3.24 us (8%)
  waiting for transfers between devices  2.1 us (5%)
    all_to_all x1, blocking collectives, local(): got = lax.all_to_all(sent, 'gy', 0, 0)  19 us
    all_to_all x1, blocking collectives, local(): got = lax.all_to_all(sent, 'gx', 0, 0)  14.2 us
    pallas_call x6, Pallas kernels, call(): pl.pallas_call(kernel, out_shape=tuple((o for o, _ in outs)), in_specs=[p...  3.95 us
    ppermute x1, starting transfers between devices, local(): lax.ppermute(high, 'gy', [(i, (i + 1) % count_y) for i in range(count_y)])  3.03 us
    ppermute x1, waiting for transfers between devices, local(): lax.ppermute(low, 'gy', [((i + 1) % count_y, i) for i in range(count_y)])  2.1 us
  transfers between devices with their start and end apart: 2, of which 1 were waited for; matrix products, arithmetic and copies ran while one was open for 0% of the time, Pallas kernels for 2%

profile of v3, /device:TPU:1, one launch (start us, length us, event | category | flops | bytes accessed | tf_op | source)
XLA Modules:
  0.0 42.5 jit_solution(13685870002432805131)
XLA Ops:
  0.0 1.2 %shard_map.28 = (f32[8,128]{1,0:T(8,128)S(1)}, f32[8,128]{1,0:T(8,128)S(1)}, f32[3,2,128,128]{3,2,1,0:T(8,128)S(1)}, f32[2,128,128]{2,1,0:T(8,128)S(1)}, f32[2,128,128]{2,1,0:T(8,128)S(1)}) custom-call(f32[3,2,128,128]{3,2,1,0:T(8,128)} %velocity_ref.1, f32[2,128,128]{2,1,0:T(8,128)} %diffusion_ref.1), custom_call_target="tpu_custom_call" | custom-call | flops 131072 | bytes 524288 | tf_op jit(solution)/shard_map/pallas_call | solution.py:483
  1.2 3.0 %collective-permute-start = (f32[8,128]{1,0:T(8,128)S(1)}, f32[8,128]{1,0:T(8,128)S(1)}, u32[]{:S(2)}, u32[]{:S(2)}) collective-permute-start(f32[8,128]{1,0:T(8,128)S(1)} %get-tuple-element.29.high_ref), channel_id=1, source_target_pairs={{0,1},{1,2},{2,3},{3,4},{4,5},{5,6},{6,7},{7,8},{8,9},{9,10},{10,1... | collective-permute-start | bytes 12296 | tf_op jit(solution)/shard_map/ppermute | solution.py:514
  4.3 0.2 collective-permute-start.1
  4.5 0.3 shard_map.29
  4.8 0.3 shard_map.30
  5.2 0.0 collective-permute-done.from_low_ref
  5.2 2.1 %collective-permute-done.1.from_high_ref = f32[8,128]{1,0:T(8,128)S(1)} collective-permute-done((f32[8,128]{1,0:T(8,128)S(1)}, f32[8,128]{1,0:T(8,128)S(1)}, u32[]{:S(2)}, u32[]{:S(2)}) %collective-permute-start.1) | collective-permute-done | bytes 4128 | tf_op jit(solution)/shard_map/ppermute | solution.py:515
  7.3 0.3 shard_map.31
  7.6 14.2 %all_to_all.10.got_ref = f32[16,17,2,128]{3,2,1,0:T(2,128)S(1)} all-to-all(f32[16,17,2,128]{3,2,1,0:T(2,128)S(1)} %get-tuple-element.41), channel_id=1, replica_groups=mesh['gx'=16,'gy'=16] {'gx'}, dimensions={0} | all-to-all | bytes 557056 | tf_op jit(solution)/shard_map/all_to_all | solution.py:554
  21.8 0.6 %shard_map.32 = (f32[16,9,2,128]{3,2,1,0:T(2,128)S(1)}, f32[6,16,8,128]{3,2,1,0:T(8,128)S(1)}, f32[6,3,8,128]{3,2,1,0:T(8,128)S(1)}, f32[16,128]{1,0:T(8,128)S(1)}) custom-call(f32[16,17,2,128]{3,2,1,0:T(2,128)S(1)} %all_to_all.10.got_ref, f32[8,128]{1,0:T(8,128)S(1)} %collective-permute-done.1.from_high_ref, ...), custom_call_target="tpu_custom_call" | custom-call | flops 4194304 | bytes 524288 | tf_op jit(solution)/shard_map/pallas_call | solution.py:483
  22.4 19.0 %all_to_all.11.got_ref = f32[16,9,2,128]{3,2,1,0:T(2,128)S(1)} all-to-all(f32[16,9,2,128]{3,2,1,0:T(2,128)S(1)} %get-tuple-element.49), channel_id=1, replica_groups=mesh['gx'=16,'gy'=16] {'gy'}, dimensions={0} | all-to-all | bytes 294912 | tf_op jit(solution)/shard_map/all_to_all | solution.py:563
  41.4 1.1 %shard_map.33 = f32[3,2,128,128]{3,2,1,0:T(8,128)} custom-call(f32[16,9,2,128]{3,2,1,0:T(2,128)S(1)} %all_to_all.11.got_ref, f32[16,128]{1,0:T(8,128)S(1)} %get-tuple-element.50.own_ref, f32[2,3,16,8,128]{4,3,2,1,0:T(8,128)S(1)} %get-tuple-element.44.cy_ref.coef_ref, f32[2,3,3,8,128]{4,3,2,1,0:T(8,128)S(1)} %get-tuple-element.45.ty_ref.tree_ref, ...), custom_call_target="tpu_custom_call" | custom-call | flops 4194304 | bytes 524288 | tf_op jit(solution)/shard_map/pallas_call | solution.py:483
Async XLA Ops:
  1.2 4.0 %collective-permute-start = (f32[8,128]{1,0:T(8,128)S(1)}, f32[8,128]{1,0:T(8,128)S(1)}, u32[]{:S(2)}, u32[]{:S(2)}) collective-permute-start(f32[8,128]{1,0:T(8,128)S(1)} %get-tuple-element.29.high_ref), channel_id=1, source_target_pairs={{0,1},{1,2},{2,3},{3,4},{4,5},{5,6},{6,7},{7,8},{8,9},{9,10},{10,1... | collective-permute-start | bytes 12296 | tf_op jit(solution)/shard_map/ppermute | solution.py:514
  4.3 3.0 %collective-permute-start.1 = (f32[8,128]{1,0:T(8,128)S(1)}, f32[8,128]{1,0:T(8,128)S(1)}, u32[]{:S(2)}, u32[]{:S(2)}) collective-permute-start(f32[8,128]{1,0:T(8,128)S(1)} %get-tuple-element.30.low_ref), channel_id=1, source_target_pairs={{1,0},{2,1},{3,2},{4,3},{5,4},{6,5},{7,6},{8,7},{9,8},{10,9},{11,1... | collective-permute-start | bytes 12296 | tf_op jit(solution)/shard_map/ppermute | solution.py:515

commit v4 on v3

--- a/solution.py
+++ b/solution.py
@@ -275,7 +275,12 @@
     ]
 
 
-def edges_kernel(velocity_ref, diffusion_ref, low_ref, high_ref, v_ref, d_ref, turn_ref, sem):
+def by_parity(even, odd):
+    return jnp.where(lax.axis_index("gy") % 2 == 0, even, odd)
+
+
+def edges_kernel(velocity_ref, diffusion_ref, low_ref, high_ref, near_ref, far_ref, v_ref, d_ref,
+                 turn_ref, sem):
     copies = [
         pltpu.make_async_copy(velocity_ref, v_ref, sem.at[0]),
         pltpu.make_async_copy(diffusion_ref, d_ref, sem.at[1]),
@@ -291,8 +296,12 @@
         else:
             turned = jnp.transpose(d_ref[k - 6])
             turn_ref[k - 6] = turned
-        low_ref[k : k + 1, :] = turned[0:1]
-        high_ref[k : k + 1, :] = turned[LANES - 1 : LANES]
+        low = turned[0:1]
+        high = turned[LANES - 1 : LANES]
+        low_ref[k : k + 1, :] = low
+        high_ref[k : k + 1, :] = high
+        near_ref[k : k + 1, :] = by_parity(high, low)
+        far_ref[k : k + 1, :] = by_parity(low, high)
 
 
 def matrix_kernel(diffusion_ref, turn_ref, low_ref, high_ref, cx_ref, tx_ref, hx_ref, cy_ref, ty_ref,
@@ -354,14 +363,16 @@
             page_ref[ROW_VHI + k : ROW_VHI + k + 1, :] = own[SEG - 1][7:8]
 
 
-def halo_kernel(count, from_low_ref, from_high_ref, vp_ref, coef_ref, tree_ref, page_ref, out_ref,
+def halo_kernel(count, from_near_ref, from_far_ref, vp_ref, coef_ref, tree_ref, page_ref, out_ref,
                 q_ref, qtree_ref, edge_ref, halo_ref):
     me_y = lax.axis_index("gy")
     count_y = lax.axis_size("gy")
     row = sub_iota()
     lane = lane_iota()
-    edge_ref[0:8, :] = jnp.where(me_y == 0, 0.0, HALF * from_low_ref[...])
-    edge_ref[8:16, :] = jnp.where(me_y == count_y - 1, 0.0, -HALF * from_high_ref[...])
+    near = from_near_ref[...]
+    far = from_far_ref[...]
+    edge_ref[0:8, :] = jnp.where(me_y == 0, 0.0, HALF * by_parity(far, near))
+    edge_ref[8:16, :] = jnp.where(me_y == count_y - 1, 0.0, -HALF * by_parity(near, far))
     edge_ref[16:, :] = jnp.zeros((LANES - 16, LANES), f32)
     halo_ref[...] = jnp.transpose(edge_ref[...])
     sources = [
@@ -384,7 +395,7 @@
             out_ref[i, j] = rows
 
 
-def middle_kernel(count_x, count_y, got_ref, from_high_ref, cx_ref, tx_ref, qx_ref, qtx_ref, cy_ref,
+def middle_kernel(count_x, count_y, got_ref, from_near_ref, from_far_ref, cx_ref, tx_ref, qx_ref, qtx_ref, cy_ref,
                   ty_ref, hy_ref, cp_ref, tp_ref, qp_ref, qtp_ref, out_ref, q_ref, qtree_ref, own_ref,
                   ring_ref, plane_ref, turn_ref, pack_ref, extra_ref):
     me = lax.axis_index("gx")
@@ -410,7 +421,8 @@
 
         g = head(ROW_G)
         leak_r = head(ROW_ER)
-        beyond = from_high_ref[6 + plane : 7 + plane, :]
+        line = slice(6 + plane, 7 + plane)
+        beyond = by_parity(from_near_ref[line, :], from_far_ref[line, :])
         f = 0.5 * (head(ROW_DHI) + jnp.where(wall, 0.0, beyond))
         inv = 1.0 / (g + f + leak_r)
         a = g * inv
@@ -496,10 +508,12 @@
     count_y = lax.axis_size("gy")
     tile = (8, LANES)
     n = COMPS * PLANES
-    low, high, cells, diff, turned = call(
+    low, high, near, far, cells, diff, turned = call(
         edges_kernel,
         (HBM, HBM),
         [
+            (shape(*tile), VMEM),
+            (shape(*tile), VMEM),
             (shape(*tile), VMEM),
             (shape(*tile), VMEM),
             (shape(COMPS, PLANES, LANES, LANES), VMEM),
@@ -511,8 +525,9 @@
         pltpu.with_memory_space_constraint(velocity, HBM),
         pltpu.with_memory_space_constraint(diffusion, HBM),
     )
-    from_low = lax.ppermute(high, "gy", [(i, (i + 1) % count_y) for i in range(count_y)])
-    from_high = lax.ppermute(low, "gy", [((i + 1) % count_y, i) for i in range(count_y)])
+    ring = range(count_y)
+    from_far = lax.ppermute(far, "gy", [(i, (i - 1 + 2 * (i % 2)) % count_y) for i in ring])
+    from_near = lax.ppermute(near, "gy", [(i, i ^ 1) for i in ring])
     coef = (shape(PLANES, 3, SEG, *tile), VMEM)
     tree = (shape(PLANES, 3, 3, *tile), VMEM)
     head = (shape(16, LANES), VMEM)
@@ -549,16 +564,16 @@
         ],
         [square, square],
         1 << 18,
-        from_low, from_high, vp, cp, tp, page,
+        from_near, from_far, vp, cp, tp, page,
     )
     got = lax.all_to_all(sent, "gx", 0, 0)
     sent, qy, qty, own = call(
         partial(middle_kernel, count_x, count_y),
-        (VMEM,) * 13,
+        (VMEM,) * 14,
         [(shape(count_y, ROWS_SENT_Y // 2, 2, LANES), VMEM), q_all, q_tree, head],
         [VMEM((count_x * ROWS_X, LANES), f32), block, block, square, square],
         1 << 22,
-        got, from_high, cx, tx, qx, qtx, cy, ty, hy, cp, tp, qp, qtp,
+        got, from_near, from_far, cx, tx, qx, qtx, cy, ty, hy, cp, tp, qp, qtp,
     )
     got = lax.all_to_all(sent, "gy", 0, 0)
     (result,) = call(

time: 42.7 us -> 42.4 us (level)
  blocking collectives: 33.2 us -> 32.7 us
    all_to_all x1, blocking collectives: 14.2 us -> 12.5 us  [local(): got = lax.all_to_all(sent, 'gx', 0, 0)]
    all_to_all x1, blocking collectives: 19 us -> 20.2 us  [local(): got = lax.all_to_all(sent, 'gy', 0, 0)]
  transfers between devices with their start and end apart: 2 -> 2, of which waited for: 1 -> 2; matrix products, arithmetic and copies ran while one was open for 0% -> 0% of each run, Pallas kernels for 2% -> 2%
where the time goes in v4:
time: 42.4 us; the launch traced here: 42.3 us
  blocking collectives  32.7 us (77%)
  Pallas kernels  3.91 us (9%)
  starting transfers between devices  3.29 us (8%)
  waiting for transfers between devices  2.31 us (5%)
    all_to_all x1, blocking collectives, local(): got = lax.all_to_all(sent, 'gy', 0, 0)  20.2 us
    all_to_all x1, blocking collectives, local(): got = lax.all_to_all(sent, 'gx', 0, 0)  12.5 us
    pallas_call x6, Pallas kernels, call(): pl.pallas_call(kernel, out_shape=tuple((o for o, _ in outs)), in_specs=[p...  3.91 us
    ppermute x1, starting transfers between devices, local(): from_near = lax.ppermute(near, 'gy', [(i, i ^ 1) for i in ring])  3.29 us
    ppermute x1, waiting for transfers between devices, local(): lax.ppermute(far, 'gy', [(i, (i - 1 + 2 * (i % 2)) % count_y) for i in ri...  2.21 us
  transfers between devices with their start and end apart: 2, of which 2 were waited for; matrix products, arithmetic and copies ran while one was open for 0% of the time, Pallas kernels for 2%

profile of v4, /device:TPU:1, one launch (start us, length us, event | category | flops | bytes accessed | tf_op | source)
XLA Modules:
  0.0 42.3 jit_solution(15985799539313885612)
XLA Ops:
  0.0 1.2 %shard_map.28 = (f32[8,128]{1,0:T(8,128)S(1)}, f32[8,128]{1,0:T(8,128)S(1)}, f32[8,128]{1,0:T(8,128)S(1)}, f32[8,128]{1,0:T(8,128)S(1)}, f32[3,2,128,128]{3,2,1,...) custom-call(f32[3,2,128,128]{3,2,1,0:T(8,128)} %velocity_ref.1, f32[2,128,128]{2,1,0:T(8,128)} %diffusion_ref.1), custom_call_target="tpu_custom_call" | custom-call | flops 131072 | bytes 524288 | tf_op jit(solution)/shard_map/pallas_call | solution.py:495
  1.2 3.3 %collective-permute-start = (f32[8,128]{1,0:T(8,128)S(1)}, f32[8,128]{1,0:T(8,128)S(1)}, u32[]{:S(2)}, u32[]{:S(2)}) collective-permute-start(f32[8,128]{1,0:T(8,128)S(1)} %get-tuple-element.31), channel_id=1, source_target_pairs={{0,1},{1,0},{2,3},{3,2},{4,5},{5,4},{6,7},{7,6},{8,9},{9,8},{10,11... | collective-permute-start | bytes 12296 | tf_op jit(solution)/shard_map/ppermute | solution.py:530
  4.5 0.0 collective-permute-start.1
  4.5 0.3 shard_map.29
  4.9 0.4 shard_map.30
  5.3 0.1 collective-permute-done.from_near_ref
  5.4 2.2 %collective-permute-done.1.from_far_ref = f32[8,128]{1,0:T(8,128)S(1)} collective-permute-done((f32[8,128]{1,0:T(8,128)S(1)}, f32[8,128]{1,0:T(8,128)S(1)}, u32[]{:S(2)}, u32[]{:S(2)}) %collective-permute-start.1) | collective-permute-done | bytes 4128 | tf_op jit(solution)/shard_map/ppermute | solution.py:529
  7.6 0.3 shard_map.31
  7.9 12.5 %all_to_all.10.got_ref = f32[16,17,2,128]{3,2,1,0:T(2,128)S(1)} all-to-all(f32[16,17,2,128]{3,2,1,0:T(2,128)S(1)} %get-tuple-element.45), channel_id=1, replica_groups=mesh['gx'=16,'gy'=16] {'gx'}, dimensions={0} | all-to-all | bytes 557056 | tf_op jit(solution)/shard_map/all_to_all | solution.py:569
  20.3 0.6 %shard_map.32 = (f32[16,9,2,128]{3,2,1,0:T(2,128)S(1)}, f32[6,16,8,128]{3,2,1,0:T(8,128)S(1)}, f32[6,3,8,128]{3,2,1,0:T(8,128)S(1)}, f32[16,128]{1,0:T(8,128)S(1)}) custom-call(f32[16,17,2,128]{3,2,1,0:T(2,128)S(1)} %all_to_all.10.got_ref, f32[8,128]{1,0:T(8,128)S(1)} %collective-permute-done.from_near_ref, ...), custom_call_target="tpu_custom_call" | custom-call | flops 4194304 | bytes 524288 | tf_op jit(solution)/shard_map/pallas_call | solution.py:495
  20.9 20.2 %all_to_all.11.got_ref = f32[16,9,2,128]{3,2,1,0:T(2,128)S(1)} all-to-all(f32[16,9,2,128]{3,2,1,0:T(2,128)S(1)} %get-tuple-element.53), channel_id=1, replica_groups=mesh['gx'=16,'gy'=16] {'gy'}, dimensions={0} | all-to-all | bytes 294912 | tf_op jit(solution)/shard_map/all_to_all | solution.py:578
  41.2 1.1 %shard_map.33 = f32[3,2,128,128]{3,2,1,0:T(8,128)} custom-call(f32[16,9,2,128]{3,2,1,0:T(2,128)S(1)} %all_to_all.11.got_ref, f32[16,128]{1,0:T(8,128)S(1)} %get-tuple-element.54.own_ref, f32[2,3,16,8,128]{4,3,2,1,0:T(8,128)S(1)} %get-tuple-element.48.cy_ref.coef_ref, f32[2,3,3,8,128]{4,3,2,1,0:T(8,128)S(1)} %get-tuple-element.49.ty_ref.tree_ref, ...), custom_call_target="tpu_custom_call" | custom-call | flops 4194304 | bytes 524288 | tf_op jit(solution)/shard_map/pallas_call | solution.py:495
Async XLA Ops:
  1.2 4.1 %collective-permute-start = (f32[8,128]{1,0:T(8,128)S(1)}, f32[8,128]{1,0:T(8,128)S(1)}, u32[]{:S(2)}, u32[]{:S(2)}) collective-permute-start(f32[8,128]{1,0:T(8,128)S(1)} %get-tuple-element.31), channel_id=1, source_target_pairs={{0,1},{1,0},{2,3},{3,2},{4,5},{5,4},{6,7},{7,6},{8,9},{9,8},{10,11... | collective-permute-start | bytes 12296 | tf_op jit(solution)/shard_map/ppermute | solution.py:530
  4.5 3.0 %collective-permute-start.1 = (f32[8,128]{1,0:T(8,128)S(1)}, f32[8,128]{1,0:T(8,128)S(1)}, u32[]{:S(2)}, u32[]{:S(2)}) collective-permute-start(f32[8,128]{1,0:T(8,128)S(1)} %get-tuple-element.32), channel_id=1, source_target_pairs={{0,15},{1,2},{2,1},{3,4},{4,3},{5,6},{6,5},{7,8},{8,7},{9,10},{10,... | collective-permute-start | bytes 12296 | tf_op jit(solution)/shard_map/ppermute | solution.py:529

commit v5 on v4

--- a/solution.py
+++ b/solution.py
@@ -14,13 +14,12 @@
 PLANES = 2
 COMPS = 3
 LANES = 128
-ROWS_X = 40
-ROWS_Y = 24
+PITCH = 18
+ROWS_X = 34
+ROWS_Y = 18
 ROW_G, ROW_EL, ROW_ER, ROW_DHI, ROW_VLO, ROW_DLO = 0, 2, 4, 6, 8, 14
-ROW_JL, ROW_JR, ROW_VHI = 16, 24, 30
-TILE_X = 2
-SENT_X = [i for i in range(0, 36, TILE_X) if i != 22]
-Y_JL, Y_JR, ROWS_SENT_Y = 6, 12, 18
+ROW_JL, ROW_JR, ROW_VHI = 16, 22, 28
+Y_JL, Y_JR = 6, 12
 OWN_A, OWN_B, OWN_Q = 0, 2, 4
 
 f32 = jnp.float32
@@ -46,6 +45,21 @@
 
 def strided(ref, lead, t):
     return ref[lead, pl.ds(t, 8, stride=SEG), :]
+
+
+def segment(t):
+    return pl.ds(t, 8, stride=PITCH)
+
+
+def natural(ref, lead):
+    starts = [PITCH * (i // 2) + 8 * (i % 2) for i in range(16)]
+    return jnp.concatenate([ref[lead, start : start + 8, :] for start in starts], 0)
+
+
+def spread(ref, lead, value):
+    for i in range(16):
+        start = PITCH * (i // 2) + 8 * (i % 2)
+        ref[lead, start : start + 8, :] = value[8 * i : 8 * i + 8]
 
 
 def factor(cells, first, coef_ref, tree_ref, head_ref, plane):
@@ -143,6 +157,27 @@
         store(t, cell)
 
 
+def send_row(out_ref, rows, which, count, value):
+    value = jnp.broadcast_to(value[0:1], (8, LANES))
+    for half in range(count // 8):
+        out_ref[pl.ds(8 * half * rows + which, 8, stride=rows), :] = value
+
+
+def reader(got_ref, rows, me):
+    turn = me & 7
+    back = (8 - turn) & 7
+    same = (sub_iota() < 8 - turn) == (me < 8)
+
+    def read(which):
+        low, high = (
+            pltpu.roll(got_ref[pl.ds(8 * half * rows + which, 8, stride=rows), :], back, 0)
+            for half in (0, 1)
+        )
+        return jnp.where(same, low, high), jnp.where(same, high, low)
+
+    return read
+
+
 def cyclic(me, half, count):
     return (me + 8 * half + sub_iota()) & (count - 1)
 
@@ -194,14 +229,11 @@
     return ends
 
 
-def solve_x(ring_ref, me, count, plane):
+def solve_x(read, me, count, plane):
     row = sub_iota()
 
-    def take(which, half):
-        return ring_ref[pl.ds(8 * half * ROWS_X + which + plane, 8, stride=ROWS_X), :]
-
     def both(which):
-        return take(which, 0), take(which, 1)
+        return read(which + plane)
 
     def before(pair, half):
         return jnp.where(row == 0, after(pair[1 - half], 1), after(pair[half], 1))
@@ -209,7 +241,13 @@
     def beyond(pair, half):
         return jnp.where(row == 7, ahead(pair[1 - half], 1), ahead(pair[half], 1))
 
+    conduct = both(ROW_G)
+    leaks_l = both(ROW_EL)
+    leaks_r = both(ROW_ER)
+    last_faces = both(ROW_DHI)
     first_faces = both(ROW_DLO)
+    lefts = [both(ROW_JL + comp * PLANES) for comp in range(COMPS)]
+    rights = [both(ROW_JR + comp * PLANES) for comp in range(COMPS)]
     low_cells = [both(ROW_VLO + comp * PLANES) for comp in range(COMPS)]
     high_cells = [both(ROW_VHI + comp * PLANES) for comp in range(COMPS)]
     blocks = []
@@ -217,10 +255,10 @@
     for half in (0, 1):
         place = cyclic(me, half, count)
         wall = place == count - 1
-        g = take(ROW_G, half)
-        leak_l = take(ROW_EL, half)
-        leak_r = take(ROW_ER, half)
-        f = 0.5 * (take(ROW_DHI, half) + jnp.where(wall, 0.0, beyond(first_faces, half)))
+        g = conduct[half]
+        leak_l = leaks_l[half]
+        leak_r = leaks_r[half]
+        f = 0.5 * (last_faces[half] + jnp.where(wall, 0.0, beyond(first_faces, half)))
         inv = 1.0 / (g + f + leak_r)
         a = g * inv
         b = f * inv
@@ -233,10 +271,8 @@
         currents = []
         terms = []
         for comp in range(COMPS):
-            left = take(ROW_JL + comp * PLANES, half)
-            right = take(ROW_JR + comp * PLANES, half)
-            left = left + up_lo * before(high_cells[comp], half)
-            right = right - up_hi * beyond(low_cells[comp], half)
+            left = lefts[comp][half] + up_lo * before(high_cells[comp], half)
+            right = rights[comp][half] - up_hi * beyond(low_cells[comp], half)
             terms.append(inv * right)
             currents.append((left + a * right, b_cut * right))
         if half == 0:
@@ -249,22 +285,19 @@
     ]
 
 
-def solve_y(ring_ref, own_ref, me, count, plane):
-    def take(which, half):
-        return ring_ref[pl.ds(8 * half * ROWS_Y + which + plane, 8, stride=ROWS_Y), :]
-
+def solve_y(read, own_ref, me, count, plane):
     def own(which):
         return own_ref[which + plane : which + plane + 1, :]
 
+    g, leak_l, leak_r = (read(which + plane) for which in (ROW_G, ROW_EL, ROW_ER))
+    lefts = [read(Y_JL + comp * PLANES + plane) for comp in range(COMPS)]
+    rights = [read(Y_JR + comp * PLANES + plane) for comp in range(COMPS)]
     blocks = [
         (
-            take(ROW_G, half),
-            take(ROW_EL, half),
-            take(ROW_ER, half),
-            [
-                (take(Y_JL + comp * PLANES, half), take(Y_JR + comp * PLANES, half))
-                for comp in range(COMPS)
-            ],
+            g[half],
+            leak_l[half],
+            leak_r[half],
+            [(lefts[comp][half], rights[comp][half]) for comp in range(COMPS)],
         )
         for half in (0, 1)
     ]
@@ -314,14 +347,16 @@
             line = base + k % PLANES
             edge_ref[i, k : k + 1, :] = low_ref[line : line + 1, :]
             edge_ref[i, 8 + k : 9 + k, :] = high_ref[line : line + 1, :]
-    vp_ref[...] = jnp.transpose(edge_ref[0])
-    pack_ref[0] = jnp.transpose(edge_ref[1])
+    for i in range(2):
+        pack_ref[i] = jnp.transpose(edge_ref[i])
+    for t in range(SEG):
+        vp_ref[t] = strided(pack_ref, 0, t)
     for plane in range(PLANES):
         cells = [strided(diffusion_ref, plane, t) for t in range(SEG)]
         factor(cells, first_x, cx_ref, tx_ref, hx_ref, plane)
         cells = [strided(turn_ref, plane, t) for t in range(SEG)]
         factor(cells, first_y, cy_ref, ty_ref, hy_ref, plane)
-    cells = [strided(pack_ref, 0, t) for t in range(SEG)]
+    cells = [strided(pack_ref, 1, t) for t in range(SEG)]
     factor(cells, first_x, cp_ref, tp_ref, None, 0)
     for ref in (hx_ref, hy_ref):
         ref[ROW_VLO : ROW_VLO + 6, :] = jnp.zeros((6, LANES), f32)
@@ -331,7 +366,7 @@
     row = sub_iota()
     lane = lane_iota()
     page_ref[0:16, :] = head_ref[...]
-    page_ref[16:, :] = jnp.zeros((ROWS_X - 16, LANES), f32)
+    page_ref[ROWS_X:, :] = jnp.zeros((40 - ROWS_X, LANES), f32)
     for plane in range(PLANES):
         cells = [
             [velocity_ref[comp, plane, pl.ds(t, 8, stride=SEG), :] for t in range(SEG)]
@@ -374,44 +409,40 @@
     edge_ref[0:8, :] = jnp.where(me_y == 0, 0.0, HALF * by_parity(far, near))
     edge_ref[8:16, :] = jnp.where(me_y == count_y - 1, 0.0, -HALF * by_parity(near, far))
     edge_ref[16:, :] = jnp.zeros((LANES - 16, LANES), f32)
-    halo_ref[...] = jnp.transpose(edge_ref[...])
+    spread(halo_ref, 0, jnp.transpose(edge_ref[...]))
     sources = [
-        vp_ref[pl.ds(t, 8, stride=SEG), :] * halo_ref[pl.ds(t, 8, stride=SEG), :]
+        vp_ref[t] * halo_ref[0, segment(t), :]
         for t in range(SEG)
     ]
     ends = condense(sources, coef_ref, tree_ref, q_ref, qtree_ref, 0, 0)
-    page = [page_ref[8 * i : 8 * i + 8, :] for i in range(ROWS_X // 8)]
+    done = {}
     for base, value in zip((ROW_JL, ROW_JR), ends):
         value = jnp.broadcast_to(value[0:1], (8, LANES))
         low = jnp.sum(jnp.where(lane == row, value, 0.0), axis=1, keepdims=True)
         high = jnp.sum(jnp.where(lane == row + 8, value, 0.0), axis=1, keepdims=True)
         extra = jnp.where(lane == 0, low, jnp.where(lane == LANES - 1, high, 0.0))
-        page[base // 8] = page[base // 8] + extra
-    for i, rows in enumerate(page):
-        edge_ref[8 * i : 8 * i + 8, :] = rows
-    for j, start in enumerate(SENT_X):
-        rows = edge_ref[start : start + TILE_X, :]
-        for i in range(count):
-            out_ref[i, j] = rows
+        for k in range(COMPS * PLANES):
+            done[base + k] = page_ref[base + k : base + k + 1, :] + extra[k : k + 1]
+    for which in range(ROWS_X):
+        value = done.get(which)
+        if value is None:
+            value = page_ref[which : which + 1, :]
+        send_row(out_ref, ROWS_X, which, count, value)
 
 
 def middle_kernel(count_x, count_y, got_ref, from_near_ref, from_far_ref, cx_ref, tx_ref, qx_ref, qtx_ref, cy_ref,
                   ty_ref, hy_ref, cp_ref, tp_ref, qp_ref, qtp_ref, out_ref, q_ref, qtree_ref, own_ref,
-                  ring_ref, plane_ref, turn_ref, pack_ref, extra_ref):
+                  plane_ref, turn_ref, pack_ref, extra_ref):
     me = lax.axis_index("gx")
 
     def store_pack(t, value):
-        pack_ref[pl.ds(t, 8, stride=SEG), :] = value
+        pack_ref[0, segment(t), :] = value
 
     nothing = jnp.zeros((8, LANES), f32)
     unfold(nothing, nothing, cp_ref, tp_ref, qp_ref, qtp_ref, 0, 0, store_pack)
-    extra_ref[...] = jnp.transpose(pack_ref[...])
+    extra_ref[...] = jnp.transpose(natural(pack_ref, 0))
     wall = lax.axis_index("gy") == count_y - 1
-    for i in range(count_x):
-        slot = (i - me + count_x) & (count_x - 1)
-        base = slot * ROWS_X
-        for j, start in enumerate(SENT_X):
-            ring_ref[pl.ds(base + start, TILE_X), :] = got_ref[i, j]
+    read = reader(got_ref, ROWS_X, me)
     own_ref[10:16, :] = jnp.zeros((6, LANES), f32)
     values = {}
     for plane in range(PLANES):
@@ -435,51 +466,46 @@
         leak_l = head(ROW_EL) + a * leak_r
         values[ROW_EL + plane] = jnp.where(wall, leak_l + through, leak_l)
         values[ROW_ER + plane] = b_cut * leak_r
-        ends = solve_x(ring_ref, me, count_x, plane)
+        ends = solve_x(read, me, count_x, plane)
         for comp in range(COMPS):
             k = comp * PLANES + plane
             low, high = ends[comp]
 
             def store(t, value):
-                plane_ref[k, pl.ds(t, 8, stride=SEG), :] = value
+                plane_ref[k, segment(t), :] = value
 
             unfold(low, high, cx_ref, tx_ref, qx_ref, qtx_ref, plane, comp, store)
-            turned = jnp.transpose(plane_ref[k])
-            turn_ref[k] = turned
+            turned = jnp.transpose(natural(plane_ref, k))
+            spread(turn_ref, k, turned)
             turn_ref[k, 0:1, :] = turned[0:1] + extra_ref[k : k + 1, :]
-            turn_ref[k, LANES - 1 :, :] = turned[LANES - 1 :] + extra_ref[8 + k : 9 + k, :]
-            sources = [strided(turn_ref, k, t) for t in range(SEG)]
+            final = PITCH * 7 + SEG - 1
+            turn_ref[k, final : final + 1, :] = turned[LANES - 1 :] + extra_ref[8 + k : 9 + k, :]
+            sources = [turn_ref[k, segment(t), :] for t in range(SEG)]
             left, right = condense(sources, cy_ref, ty_ref, q_ref, qtree_ref, plane, comp)
             right = right[0:1]
             own_ref[OWN_Q + k : OWN_Q + k + 1, :] = inv * right
             values[Y_JL + k] = left[0:1] + a * right
             values[Y_JR + k] = b_cut * right
-    for pair in range(ROWS_SENT_Y // 2):
-        rows = jnp.concatenate([values[2 * pair], values[2 * pair + 1]], 0)
-        for i in range(count_y):
-            out_ref[i, pair] = rows
-
-
-def final_kernel(count, got_ref, own_ref, coef_ref, tree_ref, q_ref, qtree_ref, out_ref, ring_ref,
-                 plane_ref, turn_ref, sem):
+    for which, value in values.items():
+        send_row(out_ref, ROWS_Y, which, count_y, value)
+
+
+def final_kernel(count, got_ref, own_ref, coef_ref, tree_ref, q_ref, qtree_ref, out_ref, plane_ref,
+                 turn_ref, sem):
     me = lax.axis_index("gy")
-    for i in range(count):
-        slot = (i - me + count) & (count - 1)
-        base = slot * ROWS_Y
-        for pair in range(ROWS_SENT_Y // 2):
-            ring_ref[pl.ds(base + 2 * pair, 2), :] = got_ref[i, pair]
+    read = reader(got_ref, ROWS_Y, me)
     copies = []
     for plane in range(PLANES):
-        ends = solve_y(ring_ref, own_ref, me, count, plane)
+        ends = solve_y(read, own_ref, me, count, plane)
         for comp in range(COMPS):
             k = comp * PLANES + plane
             low, high = ends[comp]
 
             def store(t, value):
-                plane_ref[k, pl.ds(t, 8, stride=SEG), :] = value
+                plane_ref[k, segment(t), :] = value
 
             unfold(low, high, coef_ref, tree_ref, q_ref, qtree_ref, plane, comp, store)
-            turn_ref[k] = jnp.transpose(plane_ref[k])
+            turn_ref[k] = jnp.transpose(natural(plane_ref, k))
             copy = pltpu.make_async_copy(turn_ref.at[k], out_ref.at[comp, plane], sem.at[k])
             copy.start()
             copies.append(copy)
@@ -501,6 +527,12 @@
         cost_estimate=pl.CostEstimate(flops=cost, bytes_accessed=1 << 19, transcendentals=0),
         compiler_params=pltpu.CompilerParams(vmem_limit_bytes=8 << 20),
     )(*args)
+
+
+def share(sent, axis):
+    count = lax.axis_size(axis)
+    got = lax.all_to_all(sent.reshape(count, -1, 2, LANES), axis, 0, 0)
+    return got.reshape(-1, LANES)
 
 
 def local(velocity, diffusion):
@@ -534,6 +566,7 @@
     q_all = (shape(n, SEG, *tile), VMEM)
     q_tree = (shape(n, 3, *tile), VMEM)
     block = VMEM((n, LANES, LANES), f32)
+    pitched = VMEM((n, 8 * PITCH, LANES), f32)
     square = VMEM((LANES, LANES), f32)
     pair = VMEM((PLANES, LANES, LANES), f32)
     coef_pack = (shape(1, 3, SEG, *tile), VMEM)
@@ -541,7 +574,7 @@
     cx, tx, hx, cy, ty, hy, cp, tp, vp = call(
         matrix_kernel,
         (VMEM,) * 4,
-        [coef, tree, head] * 2 + [coef_pack, tree_pack, (shape(LANES, LANES), VMEM)],
+        [coef, tree, head] * 2 + [coef_pack, tree_pack, (shape(SEG, *tile), VMEM)],
         [pair, pair],
         1 << 21,
         diff, turned, low, high,
@@ -549,7 +582,7 @@
     page, qx, qtx = call(
         source_kernel,
         (VMEM,) * 4,
-        [(shape(ROWS_X, LANES), VMEM), q_all, q_tree],
+        [(shape(40, LANES), VMEM), q_all, q_tree],
         [],
         1 << 22,
         cells, cx, tx, hx,
@@ -558,31 +591,30 @@
         partial(halo_kernel, count_x),
         (VMEM,) * 6,
         [
-            (shape(count_x, len(SENT_X), TILE_X, LANES), VMEM),
+            (shape(count_x * ROWS_X, LANES), VMEM),
             (shape(1, SEG, *tile), VMEM),
             (shape(1, 3, *tile), VMEM),
         ],
-        [square, square],
+        [square, VMEM((1, 8 * PITCH, LANES), f32)],
         1 << 18,
         from_near, from_far, vp, cp, tp, page,
     )
-    got = lax.all_to_all(sent, "gx", 0, 0)
+    got = share(sent, "gx")
     sent, qy, qty, own = call(
         partial(middle_kernel, count_x, count_y),
         (VMEM,) * 14,
-        [(shape(count_y, ROWS_SENT_Y // 2, 2, LANES), VMEM), q_all, q_tree, head],
-        [VMEM((count_x * ROWS_X, LANES), f32), block, block, square, square],
+        [(shape(count_y * ROWS_Y, LANES), VMEM), q_all, q_tree, head],
+        [pitched, pitched, VMEM((1, 8 * PITCH, LANES), f32), square],
         1 << 22,
         got, from_near, from_far, cx, tx, qx, qtx, cy, ty, hy, cp, tp, qp, qtp,
     )
-    got = lax.all_to_all(sent, "gy", 0, 0)
+    got = share(sent, "gy")
     (result,) = call(
         partial(final_kernel, count_y),
         (VMEM,) * 6,
         [(shape(COMPS, PLANES, LANES, LANES), HBM)],
         [
-            VMEM((count_y * ROWS_Y, LANES), f32),
-            block,
+            pitched,
             block,
             pltpu.SemaphoreType.DMA((n,)),
         ],

time: 42.4 us -> 42.2 us (level)
  no operation moved by 1% of the time
where the time goes in v5:
time: 42.2 us; the launch traced here: 42 us
  blocking collectives  32.7 us (77%)
  Pallas kernels  3.71 us (9%)
  starting transfers between devices  3.29 us (8%)
  waiting for transfers between devices  2.3 us (5%)
    all_to_all x2, blocking collectives, share(): got = lax.all_to_all(sent.reshape(count, -1, 2, LANES), axis, 0, 0)  32.7 us
    pallas_call x6, Pallas kernels, call(): pl.pallas_call(kernel, out_shape=tuple((o for o, _ in outs)), in_specs=[p...  3.71 us
    ppermute x1, starting transfers between devices, local(): from_near = lax.ppermute(near, 'gy', [(i, i ^ 1) for i in ring])  3.29 us
    ppermute x1, waiting for transfers between devices, local(): lax.ppermute(far, 'gy', [(i, (i - 1 + 2 * (i % 2)) % count_y) for i in ri...  2.21 us
  transfers between devices with their start and end apart: 2, of which 2 were waited for; matrix products, arithmetic and copies ran while one was open for 0% of the time, Pallas kernels for 2%

profile of v5, /device:TPU:1, one launch (start us, length us, event | category | flops | bytes accessed | tf_op | source)
XLA Modules:
  0.0 42.0 jit_solution(4476702052247579495)
XLA Ops:
  0.0 1.2 %shard_map.28 = (f32[8,128]{1,0:T(8,128)S(1)}, f32[8,128]{1,0:T(8,128)S(1)}, f32[8,128]{1,0:T(8,128)S(1)}, f32[8,128]{1,0:T(8,128)S(1)}, f32[3,2,128,128]{3,2,1,...) custom-call(f32[3,2,128,128]{3,2,1,0:T(8,128)} %velocity_ref.1, f32[2,128,128]{2,1,0:T(8,128)} %diffusion_ref.1), custom_call_target="tpu_custom_call" | custom-call | flops 131072 | bytes 524288 | tf_op jit(solution)/shard_map/pallas_call | solution.py:521
  1.2 3.3 %collective-permute-start = (f32[8,128]{1,0:T(8,128)S(1)}, f32[8,128]{1,0:T(8,128)S(1)}, u32[]{:S(2)}, u32[]{:S(2)}) collective-permute-start(f32[8,128]{1,0:T(8,128)S(1)} %get-tuple-element.31), channel_id=1, source_target_pairs={{0,1},{1,0},{2,3},{3,2},{4,5},{5,4},{6,7},{7,6},{8,9},{9,8},{10,11... | collective-permute-start | bytes 12296 | tf_op jit(solution)/shard_map/ppermute | solution.py:562
  4.5 0.0 collective-permute-start.1
  4.5 0.4 shard_map.29
  4.9 0.4 shard_map.30
  5.3 0.1 collective-permute-done.from_near_ref
  5.4 2.2 %collective-permute-done.1.from_far_ref = f32[8,128]{1,0:T(8,128)S(1)} collective-permute-done((f32[8,128]{1,0:T(8,128)S(1)}, f32[8,128]{1,0:T(8,128)S(1)}, u32[]{:S(2)}, u32[]{:S(2)}) %collective-permute-start.1) | collective-permute-done | bytes 4128 | tf_op jit(solution)/shard_map/ppermute | solution.py:561
  7.6 0.2 shard_map.31
  7.8 12.5 %all_to_all.10 = f32[16,17,2,128]{3,2,1,0:T(2,128)S(1)} all-to-all(f32[16,17,2,128]{3,2,1,0:T(2,128)S(1)} %bitcast.6), channel_id=1, replica_groups=mesh['gx'=16,'gy'=16] {'gx'}, dimensions={0} | all-to-all | bytes 557056 | tf_op jit(solution)/shard_map/all_to_all | solution.py:534
  20.3 0.5 %shard_map.32 = (f32[288,128]{1,0:T(8,128)S(1)}, f32[6,16,8,128]{3,2,1,0:T(8,128)S(1)}, f32[6,3,8,128]{3,2,1,0:T(8,128)S(1)}, f32[16,128]{1,0:T(8,128)S(1)}) custom-call(f32[544,128]{1,0:T(8,128)S(1)} %bitcast.4, f32[8,128]{1,0:T(8,128)S(1)} %collective-permute-done.from_near_ref, f32[8,128]{1,0:T(8,128)S(1)} %collective-permute-done.1.from_far_ref, ...), custom_call_target="tpu_custom_call" | custom-call | flops 4194304 | bytes 524288 | tf_op jit(solution)/shard_map/pallas_call | solution.py:521
  20.8 20.2 %all_to_all.11 = f32[16,9,2,128]{3,2,1,0:T(2,128)S(1)} all-to-all(f32[16,9,2,128]{3,2,1,0:T(2,128)S(1)} %bitcast.7), channel_id=1, replica_groups=mesh['gx'=16,'gy'=16] {'gy'}, dimensions={0} | all-to-all | bytes 294912 | tf_op jit(solution)/shard_map/all_to_all | solution.py:534
  41.0 1.0 %shard_map.33 = f32[3,2,128,128]{3,2,1,0:T(8,128)} custom-call(f32[288,128]{1,0:T(8,128)S(1)} %bitcast.5, f32[16,128]{1,0:T(8,128)S(1)} %get-tuple-element.54.own_ref, f32[2,3,16,8,128]{4,3,2,1,0:T(8,128)S(1)} %get-tuple-element.48.cy_ref.coef_ref, f32[2,3,3,8,128]{4,3,2,1,0:T(8,128)S(1)} %get-tuple-element.49.ty_ref.tree_ref, ...), custom_call_target="tpu_custom_call" | custom-call | flops 4194304 | bytes 524288 | tf_op jit(solution)/shard_map/pallas_call | solution.py:521
Async XLA Ops:
  1.2 4.1 %collective-permute-start = (f32[8,128]{1,0:T(8,128)S(1)}, f32[8,128]{1,0:T(8,128)S(1)}, u32[]{:S(2)}, u32[]{:S(2)}) collective-permute-start(f32[8,128]{1,0:T(8,128)S(1)} %get-tuple-element.31), channel_id=1, source_target_pairs={{0,1},{1,0},{2,3},{3,2},{4,5},{5,4},{6,7},{7,6},{8,9},{9,8},{10,11... | collective-permute-start | bytes 12296 | tf_op jit(solution)/shard_map/ppermute | solution.py:562
  4.5 3.0 %collective-permute-start.1 = (f32[8,128]{1,0:T(8,128)S(1)}, f32[8,128]{1,0:T(8,128)S(1)}, u32[]{:S(2)}, u32[]{:S(2)}) collective-permute-start(f32[8,128]{1,0:T(8,128)S(1)} %get-tuple-element.32), channel_id=1, source_target_pairs={{0,15},{1,2},{2,1},{3,4},{4,3},{5,6},{6,5},{7,8},{8,7},{9,10},{10,... | collective-permute-start | bytes 12296 | tf_op jit(solution)/shard_map/ppermute | solution.py:561

commit v6 on v5

--- a/solution.py
+++ b/solution.py
@@ -21,6 +21,9 @@
 ROW_JL, ROW_JR, ROW_VHI = 16, 22, 28
 Y_JL, Y_JR = 6, 12
 OWN_A, OWN_B, OWN_Q = 0, 2, 4
+
+ORDER_X = [6, 11, 15, 0, 7, 9, 12, 3, 4, 8, 13, 1, 5, 10, 14, 2]
+ORDER_Y = [11, 8, 2, 9, 7, 5, 6, 13, 14, 4, 15, 12, 10, 0, 3, 1]
 
 f32 = jnp.float32
 VMEM = pltpu.VMEM
@@ -163,17 +166,19 @@
         out_ref[pl.ds(8 * half * rows + which, 8, stride=rows), :] = value
 
 
-def reader(got_ref, rows, me):
-    turn = me & 7
-    back = (8 - turn) & 7
-    same = (sub_iota() < 8 - turn) == (me < 8)
+def reader(got_ref, ring_ref, rows, order, me):
+    count = len(order)
+    for i, source in enumerate(order):
+        base = ((source - me + count) & (count - 1)) * rows
+        for start in range(0, rows, 8):
+            size = min(8, rows - start)
+            piece = got_ref[rows * i + start : rows * i + start + size, :]
+            ring_ref[pl.ds(base + start, size), :] = piece
 
     def read(which):
-        low, high = (
-            pltpu.roll(got_ref[pl.ds(8 * half * rows + which, 8, stride=rows), :], back, 0)
-            for half in (0, 1)
+        return tuple(
+            ring_ref[pl.ds(8 * half * rows + which, 8, stride=rows), :] for half in (0, 1)
         )
-        return jnp.where(same, low, high), jnp.where(same, high, low)
 
     return read
 
@@ -432,7 +437,7 @@
 
 def middle_kernel(count_x, count_y, got_ref, from_near_ref, from_far_ref, cx_ref, tx_ref, qx_ref, qtx_ref, cy_ref,
                   ty_ref, hy_ref, cp_ref, tp_ref, qp_ref, qtp_ref, out_ref, q_ref, qtree_ref, own_ref,
-                  plane_ref, turn_ref, pack_ref, extra_ref):
+                  plane_ref, turn_ref, pack_ref, extra_ref, ring_ref):
     me = lax.axis_index("gx")
 
     def store_pack(t, value):
@@ -442,7 +447,7 @@
     unfold(nothing, nothing, cp_ref, tp_ref, qp_ref, qtp_ref, 0, 0, store_pack)
     extra_ref[...] = jnp.transpose(natural(pack_ref, 0))
     wall = lax.axis_index("gy") == count_y - 1
-    read = reader(got_ref, ROWS_X, me)
+    read = reader(got_ref, ring_ref, ROWS_X, ORDER_X, me)
     own_ref[10:16, :] = jnp.zeros((6, LANES), f32)
     values = {}
     for plane in range(PLANES):
@@ -491,9 +496,9 @@
 
 
 def final_kernel(count, got_ref, own_ref, coef_ref, tree_ref, q_ref, qtree_ref, out_ref, plane_ref,
-                 turn_ref, sem):
+                 turn_ref, ring_ref, sem):
     me = lax.axis_index("gy")
-    read = reader(got_ref, ROWS_Y, me)
+    read = reader(got_ref, ring_ref, ROWS_Y, ORDER_Y, me)
     copies = []
     for plane in range(PLANES):
         ends = solve_y(read, own_ref, me, count, plane)
@@ -529,9 +534,9 @@
     )(*args)
 
 
-def share(sent, axis):
-    count = lax.axis_size(axis)
-    got = lax.all_to_all(sent.reshape(count, -1, 2, LANES), axis, 0, 0)
+def share(sent, axis, order):
+    pages = sent.reshape(len(order), -1, 2, LANES)
+    got = lax.all_to_all(pages, axis, 0, 0, axis_index_groups=[order])
     return got.reshape(-1, LANES)
 
 
@@ -599,16 +604,22 @@
         1 << 18,
         from_near, from_far, vp, cp, tp, page,
     )
-    got = share(sent, "gx")
+    got = share(sent, "gx", ORDER_X)
     sent, qy, qty, own = call(
         partial(middle_kernel, count_x, count_y),
         (VMEM,) * 14,
         [(shape(count_y * ROWS_Y, LANES), VMEM), q_all, q_tree, head],
-        [pitched, pitched, VMEM((1, 8 * PITCH, LANES), f32), square],
+        [
+            pitched,
+            pitched,
+            VMEM((1, 8 * PITCH, LANES), f32),
+            square,
+            VMEM((count_x * ROWS_X, LANES), f32),
+        ],
         1 << 22,
         got, from_near, from_far, cx, tx, qx, qtx, cy, ty, hy, cp, tp, qp, qtp,
     )
-    got = share(sent, "gy")
+    got = share(sent, "gy", ORDER_Y)
     (result,) = call(
         partial(final_kernel, count_y),
         (VMEM,) * 6,
@@ -616,6 +627,7 @@
         [
             pitched,
             block,
+            VMEM((count_y * ROWS_Y, LANES), f32),
             pltpu.SemaphoreType.DMA((n,)),
         ],
         1 << 22,

time: 42.2 us -> 36.6 us (0.87)
  blocking collectives: 32.7 us -> 27.1 us
    all_to_all x2, blocking collectives: 32.7 us -> 27.1 us  [share(): got = lax.all_to_all(pages, axis, 0, 0, axis_index_groups=[order])]
where the time goes in v6:
time: 36.6 us; the launch traced here: 36.5 us
  blocking collectives  27.1 us (74%)
  Pallas kernels  3.74 us (10%)
  starting transfers between devices  3.29 us (9%)
  waiting for transfers between devices  2.3 us (6%)
    all_to_all x2, blocking collectives, share(): got = lax.all_to_all(pages, axis, 0, 0, axis_index_groups=[order])  27.1 us
    pallas_call x6, Pallas kernels, call(): pl.pallas_call(kernel, out_shape=tuple((o for o, _ in outs)), in_specs=[p...  3.74 us
    ppermute x1, starting transfers between devices, local(): from_near = lax.ppermute(near, 'gy', [(i, i ^ 1) for i in ring])  3.29 us
    ppermute x1, waiting for transfers between devices, local(): lax.ppermute(far, 'gy', [(i, (i - 1 + 2 * (i % 2)) % count_y) for i in ri...  2.21 us
  transfers between devices with their start and end apart: 2, of which 2 were waited for; matrix products, arithmetic and copies ran while one was open for 0% of the time, Pallas kernels for 2%

profile of v6, /device:TPU:1, one launch (start us, length us, event | category | flops | bytes accessed | tf_op | source)
XLA Modules:
  0.0 36.5 jit_solution(11591064496423400398)
XLA Ops:
  0.0 1.2 %shard_map.28 = (f32[8,128]{1,0:T(8,128)S(1)}, f32[8,128]{1,0:T(8,128)S(1)}, f32[8,128]{1,0:T(8,128)S(1)}, f32[8,128]{1,0:T(8,128)S(1)}, f32[3,2,128,128]{3,2,1,...) custom-call(f32[3,2,128,128]{3,2,1,0:T(8,128)} %velocity_ref.1, f32[2,128,128]{2,1,0:T(8,128)} %diffusion_ref.1), custom_call_target="tpu_custom_call" | custom-call | flops 131072 | bytes 524288 | tf_op jit(solution)/shard_map/pallas_call | solution.py:526
  1.2 3.3 %collective-permute-start = (f32[8,128]{1,0:T(8,128)S(1)}, f32[8,128]{1,0:T(8,128)S(1)}, u32[]{:S(2)}, u32[]{:S(2)}) collective-permute-start(f32[8,128]{1,0:T(8,128)S(1)} %get-tuple-element.31), channel_id=1, source_target_pairs={{0,1},{1,0},{2,3},{3,2},{4,5},{5,4},{6,7},{7,6},{8,9},{9,8},{10,11... | collective-permute-start | bytes 12296 | tf_op jit(solution)/shard_map/ppermute | solution.py:567
  4.5 0.0 collective-permute-start.1
  4.5 0.4 shard_map.29
  4.9 0.4 shard_map.30
  5.3 0.1 collective-permute-done.from_near_ref
  5.4 2.2 %collective-permute-done.1.from_far_ref = f32[8,128]{1,0:T(8,128)S(1)} collective-permute-done((f32[8,128]{1,0:T(8,128)S(1)}, f32[8,128]{1,0:T(8,128)S(1)}, u32[]{:S(2)}, u32[]{:S(2)}) %collective-permute-start.1) | collective-permute-done | bytes 4128 | tf_op jit(solution)/shard_map/ppermute | solution.py:566
  7.6 0.2 shard_map.31
  7.8 10.5 %all_to_all.10 = f32[16,17,2,128]{3,2,1,0:T(2,128)S(1)} all-to-all(f32[16,17,2,128]{3,2,1,0:T(2,128)S(1)} %bitcast.6), channel_id=1, replica_groups={{96,176,240,0,112,144,192,48,64,128,208,16,80,160,224,32},{97,177,241,1..., dimensions={0} | all-to-all | bytes 557056 | tf_op jit(solution)/shard_map/all_to_all | solution.py:539
  18.3 0.5 %shard_map.32 = (f32[288,128]{1,0:T(8,128)S(1)}, f32[6,16,8,128]{3,2,1,0:T(8,128)S(1)}, f32[6,3,8,128]{3,2,1,0:T(8,128)S(1)}, f32[16,128]{1,0:T(8,128)S(1)}) custom-call(f32[544,128]{1,0:T(8,128)S(1)} %bitcast.4, f32[8,128]{1,0:T(8,128)S(1)} %collective-permute-done.from_near_ref, f32[8,128]{1,0:T(8,128)S(1)} %collective-permute-done.1.from_far_ref, ...), custom_call_target="tpu_custom_call" | custom-call | flops 4194304 | bytes 524288 | tf_op jit(solution)/shard_map/pallas_call | solution.py:526
  18.7 16.6 %all_to_all.11 = f32[16,9,2,128]{3,2,1,0:T(2,128)S(1)} all-to-all(f32[16,9,2,128]{3,2,1,0:T(2,128)S(1)} %bitcast.7), channel_id=1, replica_groups={{11,8,2,9,7,5,6,13,14,4,15,12,10,0,3,1},{27,24,18,25,23,21,22,29,30,20,..., dimensions={0} | all-to-all | bytes 294912 | tf_op jit(solution)/shard_map/all_to_all | solution.py:539
  35.4 1.1 %shard_map.33 = f32[3,2,128,128]{3,2,1,0:T(8,128)} custom-call(f32[288,128]{1,0:T(8,128)S(1)} %bitcast.5, f32[16,128]{1,0:T(8,128)S(1)} %get-tuple-element.54.own_ref, f32[2,3,16,8,128]{4,3,2,1,0:T(8,128)S(1)} %get-tuple-element.48.cy_ref.coef_ref, f32[2,3,3,8,128]{4,3,2,1,0:T(8,128)S(1)} %get-tuple-element.49.ty_ref.tree_ref, ...), custom_call_target="tpu_custom_call" | custom-call | flops 4194304 | bytes 524288 | tf_op jit(solution)/shard_map/pallas_call | solution.py:526
Async XLA Ops:
  1.2 4.1 %collective-permute-start = (f32[8,128]{1,0:T(8,128)S(1)}, f32[8,128]{1,0:T(8,128)S(1)}, u32[]{:S(2)}, u32[]{:S(2)}) collective-permute-start(f32[8,128]{1,0:T(8,128)S(1)} %get-tuple-element.31), channel_id=1, source_target_pairs={{0,1},{1,0},{2,3},{3,2},{4,5},{5,4},{6,7},{7,6},{8,9},{9,8},{10,11... | collective-permute-start | bytes 12296 | tf_op jit(solution)/shard_map/ppermute | solution.py:567
  4.5 3.0 %collective-permute-start.1 = (f32[8,128]{1,0:T(8,128)S(1)}, f32[8,128]{1,0:T(8,128)S(1)}, u32[]{:S(2)}, u32[]{:S(2)}) collective-permute-start(f32[8,128]{1,0:T(8,128)S(1)} %get-tuple-element.32), channel_id=1, source_target_pairs={{0,15},{1,2},{2,1},{3,4},{4,3},{5,6},{6,5},{7,8},{8,7},{9,10},{10,... | collective-permute-start | bytes 12296 | tf_op jit(solution)/shard_map/ppermute | solution.py:566

commit v7 on v6

--- a/solution.py
+++ b/solution.py
@@ -22,8 +22,8 @@
 Y_JL, Y_JR = 6, 12
 OWN_A, OWN_B, OWN_Q = 0, 2, 4
 
-ORDER_X = [6, 11, 15, 0, 7, 9, 12, 3, 4, 8, 13, 1, 5, 10, 14, 2]
-ORDER_Y = [11, 8, 2, 9, 7, 5, 6, 13, 14, 4, 15, 12, 10, 0, 3, 1]
+ORDER_X = [14, 3, 10, 8, 7, 0, 2, 15, 5, 4, 9, 11, 13, 12, 6, 1]
+ORDER_Y = [13, 15, 1, 0, 3, 14, 6, 11, 2, 12, 7, 10, 8, 9, 4, 5]
 
 f32 = jnp.float32
 VMEM = pltpu.VMEM

time: 36.6 us -> 35 us (0.956); the launches traced: 36.5 us -> 34.4 us
  blocking collectives: 27.1 us -> 25.1 us
    all_to_all x2, blocking collectives: 27.1 us -> 25.1 us  [share(): got = lax.all_to_all(pages, axis, 0, 0, axis_index_groups=[order])]
where the time goes in v7:
time: 35 us; the launch traced here: 34.4 us
  blocking collectives  25.1 us (72%)
  Pallas kernels  3.74 us (11%)
  starting transfers between devices  3.29 us (9%)
  waiting for transfers between devices  2.3 us (7%)
    all_to_all x2, blocking collectives, share(): got = lax.all_to_all(pages, axis, 0, 0, axis_index_groups=[order])  25.1 us
    pallas_call x6, Pallas kernels, call(): pl.pallas_call(kernel, out_shape=tuple((o for o, _ in outs)), in_specs=[p...  3.74 us
    ppermute x1, starting transfers between devices, local(): from_near = lax.ppermute(near, 'gy', [(i, i ^ 1) for i in ring])  3.29 us
    ppermute x1, waiting for transfers between devices, local(): lax.ppermute(far, 'gy', [(i, (i - 1 + 2 * (i % 2)) % count_y) for i in ri...  2.21 us
  transfers between devices with their start and end apart: 2, of which 2 were waited for; matrix products, arithmetic and copies ran while one was open for 0% of the time, Pallas kernels for 2%

profile of v7, /device:TPU:1, one launch (start us, length us, event | category | flops | bytes accessed | tf_op | source)
XLA Modules:
  0.0 34.4 jit_solution(12003832894760589573)
XLA Ops:
  0.0 1.2 %shard_map.28 = (f32[8,128]{1,0:T(8,128)S(1)}, f32[8,128]{1,0:T(8,128)S(1)}, f32[8,128]{1,0:T(8,128)S(1)}, f32[8,128]{1,0:T(8,128)S(1)}, f32[3,2,128,128]{3,2,1,...) custom-call(f32[3,2,128,128]{3,2,1,0:T(8,128)} %velocity_ref.1, f32[2,128,128]{2,1,0:T(8,128)} %diffusion_ref.1), custom_call_target="tpu_custom_call" | custom-call | flops 131072 | bytes 524288 | tf_op jit(solution)/shard_map/pallas_call | solution.py:526
  1.2 3.3 %collective-permute-start = (f32[8,128]{1,0:T(8,128)S(1)}, f32[8,128]{1,0:T(8,128)S(1)}, u32[]{:S(2)}, u32[]{:S(2)}) collective-permute-start(f32[8,128]{1,0:T(8,128)S(1)} %get-tuple-element.31), channel_id=1, source_target_pairs={{0,1},{1,0},{2,3},{3,2},{4,5},{5,4},{6,7},{7,6},{8,9},{9,8},{10,11... | collective-permute-start | bytes 12296 | tf_op jit(solution)/shard_map/ppermute | solution.py:567
  4.5 0.0 collective-permute-start.1
  4.5 0.4 %shard_map.29 = (f32[2,3,16,8,128]{4,3,2,1,0:T(8,128)S(1)}, f32[2,3,3,8,128]{4,3,2,1,0:T(8,128)S(1)}, f32[16,128]{1,0:T(8,128)S(1)}, f32[2,3,16,8,128]{4,3,2,1,0...) custom-call(f32[2,128,128]{2,1,0:T(8,128)S(1)} %get-tuple-element.33, ...), custom_call_target="tpu_custom_call" | custom-call | flops 2097152 | bytes 524288 | tf_op jit(solution)/shard_map/pallas_call | solution.py:526
  4.9 0.4 %shard_map.30 = (f32[40,128]{1,0:T(8,128)S(1)}, f32[6,16,8,128]{3,2,1,0:T(8,128)S(1)}, f32[6,3,8,128]{3,2,1,0:T(8,128)S(1)}) custom-call(f32[3,2,128,128]{3,2,1,0:T(8,128)S(1)} %get-tuple-element.40.velocity_ref, f32[2,3,16,8,128]{4,3,2,1,0:T(8,128)S(1)} %get-tuple-element.41.coef_ref.cx_ref, f32[2,3,3,8,128]{4,3,2,1,0:T(8,128)S(1)} %get-tuple-element.42.tree_ref.tx_ref, ...), custom_call_target="tpu_custom_call" | custom-call | flops 4194304 | bytes 524288 | tf_op jit(solution)/shard_map/pallas_call | solution.py:526
  5.3 0.1 collective-permute-done.from_near_ref
  5.4 2.2 %collective-permute-done.1.from_far_ref = f32[8,128]{1,0:T(8,128)S(1)} collective-permute-done((f32[8,128]{1,0:T(8,128)S(1)}, f32[8,128]{1,0:T(8,128)S(1)}, u32[]{:S(2)}, u32[]{:S(2)}) %collective-permute-start.1) | collective-permute-done | bytes 4128 | tf_op jit(solution)/shard_map/ppermute | solution.py:566
  7.6 0.2 shard_map.31
  7.8 9.5 %all_to_all.10 = f32[16,17,2,128]{3,2,1,0:T(2,128)S(1)} all-to-all(f32[16,17,2,128]{3,2,1,0:T(2,128)S(1)} %bitcast.6), channel_id=1, replica_groups={{224,48,160,128,112,0,32,240,80,64,144,176,208,192,96,16},{225,49,161,1..., dimensions={0} | all-to-all | bytes 557056 | tf_op jit(solution)/shard_map/all_to_all | solution.py:539
  17.3 0.5 %shard_map.32 = (f32[288,128]{1,0:T(8,128)S(1)}, f32[6,16,8,128]{3,2,1,0:T(8,128)S(1)}, f32[6,3,8,128]{3,2,1,0:T(8,128)S(1)}, f32[16,128]{1,0:T(8,128)S(1)}) custom-call(f32[544,128]{1,0:T(8,128)S(1)} %bitcast.4, f32[8,128]{1,0:T(8,128)S(1)} %collective-permute-done.from_near_ref, f32[8,128]{1,0:T(8,128)S(1)} %collective-permute-done.1.from_far_ref, ...), custom_call_target="tpu_custom_call" | custom-call | flops 4194304 | bytes 524288 | tf_op jit(solution)/shard_map/pallas_call | solution.py:526
  17.8 15.6 %all_to_all.11 = f32[16,9,2,128]{3,2,1,0:T(2,128)S(1)} all-to-all(f32[16,9,2,128]{3,2,1,0:T(2,128)S(1)} %bitcast.7), channel_id=1, replica_groups={{13,15,1,0,3,14,6,11,2,12,7,10,8,9,4,5},{29,31,17,16,19,30,22,27,18,28,..., dimensions={0} | all-to-all | bytes 294912 | tf_op jit(solution)/shard_map/all_to_all | solution.py:539
  33.4 1.1 %shard_map.33 = f32[3,2,128,128]{3,2,1,0:T(8,128)} custom-call(f32[288,128]{1,0:T(8,128)S(1)} %bitcast.5, f32[16,128]{1,0:T(8,128)S(1)} %get-tuple-element.54.own_ref, f32[2,3,16,8,128]{4,3,2,1,0:T(8,128)S(1)} %get-tuple-element.48.cy_ref.coef_ref, f32[2,3,3,8,128]{4,3,2,1,0:T(8,128)S(1)} %get-tuple-element.49.ty_ref.tree_ref, ...), custom_call_target="tpu_custom_call" | custom-call | flops 4194304 | bytes 524288 | tf_op jit(solution)/shard_map/pallas_call | solution.py:526
Async XLA Ops:
  1.2 4.1 %collective-permute-start = (f32[8,128]{1,0:T(8,128)S(1)}, f32[8,128]{1,0:T(8,128)S(1)}, u32[]{:S(2)}, u32[]{:S(2)}) collective-permute-start(f32[8,128]{1,0:T(8,128)S(1)} %get-tuple-element.31), channel_id=1, source_target_pairs={{0,1},{1,0},{2,3},{3,2},{4,5},{5,4},{6,7},{7,6},{8,9},{9,8},{10,11... | collective-permute-start | bytes 12296 | tf_op jit(solution)/shard_map/ppermute | solution.py:567
  4.5 3.0 %collective-permute-start.1 = (f32[8,128]{1,0:T(8,128)S(1)}, f32[8,128]{1,0:T(8,128)S(1)}, u32[]{:S(2)}, u32[]{:S(2)}) collective-permute-start(f32[8,128]{1,0:T(8,128)S(1)} %get-tuple-element.32), channel_id=1, source_target_pairs={{0,15},{1,2},{2,1},{3,4},{4,3},{5,6},{6,5},{7,8},{8,7},{9,10},{10,... | collective-permute-start | bytes 12296 | tf_op jit(solution)/shard_map/ppermute | solution.py:566

commit v8 on v7

--- a/solution.py
+++ b/solution.py
@@ -22,8 +22,8 @@
 Y_JL, Y_JR = 6, 12
 OWN_A, OWN_B, OWN_Q = 0, 2, 4
 
-ORDER_X = [14, 3, 10, 8, 7, 0, 2, 15, 5, 4, 9, 11, 13, 12, 6, 1]
-ORDER_Y = [13, 15, 1, 0, 3, 14, 6, 11, 2, 12, 7, 10, 8, 9, 4, 5]
+ORDER_X = [10, 12, 14, 3, 7, 1, 13, 15, 5, 8, 11, 6, 4, 9, 0, 2]
+ORDER_Y = [13, 0, 1, 15, 3, 14, 6, 11, 2, 12, 7, 10, 8, 9, 4, 5]
 
 f32 = jnp.float32
 VMEM = pltpu.VMEM

time: 35 us -> 34.3 us (0.980)
  blocking collectives: 25.1 us -> 24.6 us
    all_to_all x2, blocking collectives: 25.1 us -> 24.6 us  [share(): got = lax.all_to_all(pages, axis, 0, 0, axis_index_groups=[order])]
where the time goes in v8:
time: 34.3 us; the launch traced here: 34 us
  blocking collectives  24.6 us (72%)
  Pallas kernels  3.74 us (11%)
  starting transfers between devices  3.29 us (10%)
  waiting for transfers between devices  2.3 us (7%)
    all_to_all x2, blocking collectives, share(): got = lax.all_to_all(pages, axis, 0, 0, axis_index_groups=[order])  24.6 us
    pallas_call x6, Pallas kernels, call(): pl.pallas_call(kernel, out_shape=tuple((o for o, _ in outs)), in_specs=[p...  3.74 us
    ppermute x1, starting transfers between devices, local(): from_near = lax.ppermute(near, 'gy', [(i, i ^ 1) for i in ring])  3.29 us
    ppermute x1, waiting for transfers between devices, local(): lax.ppermute(far, 'gy', [(i, (i - 1 + 2 * (i % 2)) % count_y) for i in ri...  2.21 us
  transfers between devices with their start and end apart: 2, of which 2 were waited for; matrix products, arithmetic and copies ran while one was open for 0% of the time, Pallas kernels for 2%

profile of v8, /device:TPU:1, one launch (start us, length us, event | category | flops | bytes accessed | tf_op | source)
XLA Modules:
  0.0 34.0 jit_solution(13922108198218036420)
XLA Ops:
  0.0 1.2 %shard_map.28 = (f32[8,128]{1,0:T(8,128)S(1)}, f32[8,128]{1,0:T(8,128)S(1)}, f32[8,128]{1,0:T(8,128)S(1)}, f32[8,128]{1,0:T(8,128)S(1)}, f32[3,2,128,128]{3,2,1,...) custom-call(f32[3,2,128,128]{3,2,1,0:T(8,128)} %velocity_ref.1, f32[2,128,128]{2,1,0:T(8,128)} %diffusion_ref.1), custom_call_target="tpu_custom_call" | custom-call | flops 131072 | bytes 524288 | tf_op jit(solution)/shard_map/pallas_call | solution.py:526
  1.2 3.3 %collective-permute-start = (f32[8,128]{1,0:T(8,128)S(1)}, f32[8,128]{1,0:T(8,128)S(1)}, u32[]{:S(2)}, u32[]{:S(2)}) collective-permute-start(f32[8,128]{1,0:T(8,128)S(1)} %get-tuple-element.31), channel_id=1, source_target_pairs={{0,1},{1,0},{2,3},{3,2},{4,5},{5,4},{6,7},{7,6},{8,9},{9,8},{10,11... | collective-permute-start | bytes 12296 | tf_op jit(solution)/shard_map/ppermute | solution.py:567
  4.5 0.0 collective-permute-start.1
  4.5 0.4 %shard_map.29 = (f32[2,3,16,8,128]{4,3,2,1,0:T(8,128)S(1)}, f32[2,3,3,8,128]{4,3,2,1,0:T(8,128)S(1)}, f32[16,128]{1,0:T(8,128)S(1)}, f32[2,3,16,8,128]{4,3,2,1,0...) custom-call(f32[2,128,128]{2,1,0:T(8,128)S(1)} %get-tuple-element.33, ...), custom_call_target="tpu_custom_call" | custom-call | flops 2097152 | bytes 524288 | tf_op jit(solution)/shard_map/pallas_call | solution.py:526
  4.9 0.4 %shard_map.30 = (f32[40,128]{1,0:T(8,128)S(1)}, f32[6,16,8,128]{3,2,1,0:T(8,128)S(1)}, f32[6,3,8,128]{3,2,1,0:T(8,128)S(1)}) custom-call(f32[3,2,128,128]{3,2,1,0:T(8,128)S(1)} %get-tuple-element.40.velocity_ref, f32[2,3,16,8,128]{4,3,2,1,0:T(8,128)S(1)} %get-tuple-element.41.coef_ref.cx_ref, f32[2,3,3,8,128]{4,3,2,1,0:T(8,128)S(1)} %get-tuple-element.42.tree_ref.tx_ref, ...), custom_call_target="tpu_custom_call" | custom-call | flops 4194304 | bytes 524288 | tf_op jit(solution)/shard_map/pallas_call | solution.py:526
  5.3 0.1 collective-permute-done.from_near_ref
  5.4 2.2 %collective-permute-done.1.from_far_ref = f32[8,128]{1,0:T(8,128)S(1)} collective-permute-done((f32[8,128]{1,0:T(8,128)S(1)}, f32[8,128]{1,0:T(8,128)S(1)}, u32[]{:S(2)}, u32[]{:S(2)}) %collective-permute-start.1) | collective-permute-done | bytes 4128 | tf_op jit(solution)/shard_map/ppermute | solution.py:566
  7.6 0.2 shard_map.31
  7.8 9.2 %all_to_all.10 = f32[16,17,2,128]{3,2,1,0:T(2,128)S(1)} all-to-all(f32[16,17,2,128]{3,2,1,0:T(2,128)S(1)} %bitcast.6), channel_id=1, replica_groups={{160,192,224,48,112,16,208,240,80,128,176,96,64,144,0,32},{161,193,225,..., dimensions={0} | all-to-all | bytes 557056 | tf_op jit(solution)/shard_map/all_to_all | solution.py:539
  17.0 0.5 %shard_map.32 = (f32[288,128]{1,0:T(8,128)S(1)}, f32[6,16,8,128]{3,2,1,0:T(8,128)S(1)}, f32[6,3,8,128]{3,2,1,0:T(8,128)S(1)}, f32[16,128]{1,0:T(8,128)S(1)}) custom-call(f32[544,128]{1,0:T(8,128)S(1)} %bitcast.4, f32[8,128]{1,0:T(8,128)S(1)} %collective-permute-done.from_near_ref, f32[8,128]{1,0:T(8,128)S(1)} %collective-permute-done.1.from_far_ref, ...), custom_call_target="tpu_custom_call" | custom-call | flops 4194304 | bytes 524288 | tf_op jit(solution)/shard_map/pallas_call | solution.py:526
  17.5 15.4 %all_to_all.11 = f32[16,9,2,128]{3,2,1,0:T(2,128)S(1)} all-to-all(f32[16,9,2,128]{3,2,1,0:T(2,128)S(1)} %bitcast.7), channel_id=1, replica_groups={{13,0,1,15,3,14,6,11,2,12,7,10,8,9,4,5},{29,16,17,31,19,30,22,27,18,28,..., dimensions={0} | all-to-all | bytes 294912 | tf_op jit(solution)/shard_map/all_to_all | solution.py:539
  32.9 1.1 %shard_map.33 = f32[3,2,128,128]{3,2,1,0:T(8,128)} custom-call(f32[288,128]{1,0:T(8,128)S(1)} %bitcast.5, f32[16,128]{1,0:T(8,128)S(1)} %get-tuple-element.54.own_ref, f32[2,3,16,8,128]{4,3,2,1,0:T(8,128)S(1)} %get-tuple-element.48.cy_ref.coef_ref, f32[2,3,3,8,128]{4,3,2,1,0:T(8,128)S(1)} %get-tuple-element.49.ty_ref.tree_ref, ...), custom_call_target="tpu_custom_call" | custom-call | flops 4194304 | bytes 524288 | tf_op jit(solution)/shard_map/pallas_call | solution.py:526
Async XLA Ops:
  1.2 4.1 %collective-permute-start = (f32[8,128]{1,0:T(8,128)S(1)}, f32[8,128]{1,0:T(8,128)S(1)}, u32[]{:S(2)}, u32[]{:S(2)}) collective-permute-start(f32[8,128]{1,0:T(8,128)S(1)} %get-tuple-element.31), channel_id=1, source_target_pairs={{0,1},{1,0},{2,3},{3,2},{4,5},{5,4},{6,7},{7,6},{8,9},{9,8},{10,11... | collective-permute-start | bytes 12296 | tf_op jit(solution)/shard_map/ppermute | solution.py:567
  4.5 3.0 %collective-permute-start.1 = (f32[8,128]{1,0:T(8,128)S(1)}, f32[8,128]{1,0:T(8,128)S(1)}, u32[]{:S(2)}, u32[]{:S(2)}) collective-permute-start(f32[8,128]{1,0:T(8,128)S(1)} %get-tuple-element.32), channel_id=1, source_target_pairs={{0,15},{1,2},{2,1},{3,4},{4,3},{5,6},{6,5},{7,8},{8,7},{9,10},{10,... | collective-permute-start | bytes 12296 | tf_op jit(solution)/shard_map/ppermute | solution.py:566
